TPU v7x, 256 devices: a whole 4x4x8 slice. The times are simulated.
256 devices in a mesh: batch: 16 (over z_hi, x, core), patch: 16 (over y, z_lo).
Axes of the slice: x: 4, y: 4, z: 8 (z_hi: 2, z_lo: 4; z = z_hi * 4 + z_lo), core: 2. Of those that a mesh axis runs over, the one named last changes fastest.
Arguments:
- latent: bfloat16 [512, 64, 1280], P(('batch', 'patch')), parts along dimension 0, may hold values from -100 to 100
- conv_weight: bfloat16 [3, 3, 1280, 1280], P(None, None, 'patch'), may hold values from -0.25 to 0.25
- channel_bias: float32 [1280], P('patch'), may hold values from -6 to 6
- w_query: bfloat16 [1280, 1280], P('patch'), may hold values from -0.5 to 0.5
- w_key: bfloat16 [1280, 1280], P('patch'), may hold values from -0.5 to 0.5
- w_value: bfloat16 [1280, 1280], P('patch'), may hold values from -0.15625 to 0.15625
- w_out: bfloat16 [1280, 1280], P('patch'), may hold values from -0.15625 to 0.15625
Outputs:
- output: bfloat16 [512, 64, 1280], P(('batch', 'patch')), parts along dimension 0
There are 16 independent parts, one for each index of `batch`. A program takes and returns all parts, laid end to end along the dimension named above; an argument that names none is the same for every part. Nothing has to cross between parts.
All inputs are finite; a program needn't handle non-finite values.
Results may differ from a plain program's by a relative error of at most 0.015.
Values may be sent and summed in bfloat16 or wider, within the bound.
A program may use at most 128 MiB of HBM per device.

v0:
```python
import jax
import jax.numpy as jnp
from jax import lax
from jax.sharding import PartitionSpec as P

C = 1280
HEADS = 20
HEAD_DIM = 64
GROUPS = 32


epsilon = 1e-05


def contract(left, right):
    return lax.dot_general(
        left, right, (((1,), (1,)), ((), ())), preferred_element_type=jnp.float32
    )


def group_norm(values, entries):
    grouped = values.reshape(-1, GROUPS, C // GROUPS)
    centre = lax.psum(jnp.sum(grouped, axis=(0, 2)), "patch") / entries
    deviation = grouped - centre[None, :, None]
    spread = lax.psum(jnp.sum(jnp.square(deviation), axis=(0, 2)), "patch") / entries
    normalized = (grouped - centre[None, :, None]) * lax.rsqrt(spread + epsilon)[None, :, None]
    return normalized.reshape(values.shape)


def convolve(padded, kernel, row_count, columns):
    running = jnp.zeros((row_count * columns, kernel.shape[2]), jnp.float32)
    for row_shift in range(3):
        for col_shift in range(3):
            window = padded[
                row_shift : row_shift + row_count, col_shift : col_shift + columns, :
            ].reshape(-1, C)
            running = running + contract(window, kernel[row_shift, col_shift])
    return running


def attend(queries, key_all, value_all):
    query_heads = queries.reshape(-1, HEADS, HEAD_DIM).transpose(1, 0, 2)
    key_heads = key_all.reshape(-1, HEADS, HEAD_DIM).transpose(1, 0, 2)
    value_heads = value_all.reshape(-1, HEADS, HEAD_DIM).transpose(1, 0, 2)

    def one_head(triple):
        query_one, key_one, value_one = triple
        scores = jnp.dot(query_one, key_one.T, preferred_element_type=jnp.float32) * HEAD_DIM ** (
            -0.5
        )
        row_peak = jnp.max(scores, axis=1, keepdims=True)
        unnormalized = jnp.exp(scores - row_peak)
        row_total = jnp.sum(unnormalized, axis=1, keepdims=True)
        mixture = jnp.dot(
            unnormalized.astype(jnp.bfloat16), value_one, preferred_element_type=jnp.float32
        )
        return mixture / row_total

    heads_out = lax.map(one_head, (query_heads, key_heads, value_heads))
    return heads_out.transpose(1, 0, 2).reshape(-1, C).astype(jnp.bfloat16)


def on_device(latent, conv_weight, channel_bias, w_query, w_key, w_value, w_out):
    rows_local, columns, channels = latent.shape
    devices = lax.axis_size("patch")
    entries = rows_local * devices * columns * (channels // GROUPS)
    inputs = latent.astype(jnp.float32)
    activated = jax.nn.silu(group_norm(inputs, entries)).astype(jnp.bfloat16)
    whole_image = lax.all_gather(activated, "patch", axis=0, tiled=True)
    all_rows = whole_image.shape[0]
    padded = jnp.pad(whole_image, ((1, 1), (1, 1), (0, 0)))
    convolved = convolve(padded, conv_weight, all_rows, columns) + channel_bias
    convolved = convolved.reshape(all_rows, columns, -1)
    returned = lax.all_to_all(
        convolved.astype(jnp.bfloat16), "patch", split_axis=0, concat_axis=2, tiled=True
    ).astype(convolved.dtype)
    hidden = (inputs + returned).astype(jnp.bfloat16)
    hidden = lax.optimization_barrier(hidden)
    residual = hidden.astype(jnp.float32).reshape(-1, channels)
    normed = group_norm(residual, entries).astype(jnp.bfloat16)
    full_query, full_key, full_value = (
        lax.all_gather(w_query, "patch", axis=0, tiled=True),
        lax.all_gather(w_key, "patch", axis=0, tiled=True),
        lax.all_gather(w_value, "patch", axis=0, tiled=True),
    )
    queries = contract(normed, full_query).astype(jnp.bfloat16)
    key_local = contract(normed, full_key).astype(jnp.bfloat16)
    value_local = contract(normed, full_value).astype(jnp.bfloat16)
    key_all, value_all = (
        lax.all_gather(key_local, "patch", axis=0, tiled=True),
        lax.all_gather(value_local, "patch", axis=0, tiled=True),
    )
    attended = attend(queries, key_all, value_all)
    projected = contract(attended, lax.all_gather(w_out, "patch", axis=0, tiled=True))
    output = (residual + projected).astype(jnp.bfloat16)
    return output.reshape(rows_local, columns, channels)


def solution(mesh):
    return jax.shard_map(
        on_device,
        mesh=mesh,
        in_specs=(
            P(("batch", "patch"), None, None),
            P(None, None, "patch", None),
            P("patch"),
            P("patch", None),
            P("patch", None),
            P("patch", None),
            P("patch", None),
        ),
        out_specs=P(("batch", "patch"), None, None),
        check_vma=False,
    )
```

profile of v0, /device:TPU:8, one launch (start us, length us, event | category | flops | bytes accessed | tf_op | source)
XLA Modules:
  0.0 840.8 jit_solution(9786328990870894424)
XLA Ops:
  7.8 37.9 %psum.28 = f32[32]{0:T(128)S(1)} all-reduce(f32[32]{0:T(128)S(1)} %reduce_sum.59), channel_id=1, replica_groups=mesh['batch'=16,'patch'=16] {'patch'}, use_global_device_ids=true, to_apply=%region_2.0 | all-reduce | flops 32 | bytes 256 | tf_op jit(solution)/shard_map/psum | solution.py:23
  47.1 38.0 %psum.29 = f32[32]{0:T(128)S(1)} all-reduce(f32[32]{0:T(128)S(1)} %reduce_sum.62), channel_id=1, replica_groups=mesh['batch'=16,'patch'=16] {'patch'}, use_global_device_ids=true, to_apply=%region_5.6 | all-reduce | flops 32 | bytes 256 | tf_op jit(solution)/shard_map/psum | solution.py:25
  85.3 1.9 fusion.24
  89.4 123.9 %all-gather.8.cloned.1.call-done = bf16[32,64,1280]{2,1,0:T(8,128)(2,1)} async-done(((bf16[2,64,1280]{2,1,0:T(8,128)(2,1)}), bf16[32,64,1280]{2,1,0:T(8,128)(2,1)}) %all-gather.8.cloned.1.call-update) | async-done | bytes 5242896 | tf_op jit(solution)/shard_map/all_gather | solution.py:69
  213.3 31.0 %pad_slice_fusion = (bf16[32,64,1280]{2,1,0:T(8,128)(2,1)S(1)}, bf16[32,64,1280]{2,1,0:T(8,128)(2,1)}, bf16[32,64,1280]{2,1,0:T(8,128)(2,1)}, bf16[32,64,1280]{2...) fusion(bf16[32,64,1280]{2,1,0:T(8,128)(2,1)} %all-gather.8.clon, ...), kind=kLoop, calls=%fused_computation.16 | loop fusion | bytes 47185920 | tf_op jit(solution)/shard_map/slice | solution.py:34
  244.3 4.4 fusion.37
  248.7 1.7 convolution_add_fusion.8
  251.2 1.7 convolution_add_fusion.7
  253.0 1.7 convolution_add_fusion.6
  255.1 1.7 convolution_add_fusion.5
  256.9 1.7 convolution_add_fusion.4
  258.6 1.7 convolution_add_fusion.3
  260.3 1.7 convolution_add_fusion.2
  262.0 1.7 fusion.16
  264.0 31.8 %all_to_all.4 = bf16[32,64,80]{2,1,0:T(8,128)(2,1)S(1)} all-to-all(bf16[32,64,80]{2,1,0:T(8,128)(2,1)S(1)} %bitcast.133), channel_id=1, replica_groups=mesh['batch'=16,'patch'=16] {'patch'}, dimensions={0} | all-to-all | bytes 655360 | tf_op jit(solution)/shard_map/all_to_all | solution.py:74
  297.0 36.3 %psum.30 = f32[32]{0:T(128)S(1)} all-reduce(f32[32]{0:T(128)S(1)} %reduce_sum.81), channel_id=1, replica_groups=mesh['batch'=16,'patch'=16] {'patch'}, use_global_device_ids=true, to_apply=%region_8.9 | all-reduce | flops 32 | bytes 256 | tf_op jit(solution)/shard_map/psum | solution.py:23
  333.8 40.2 %psum.31 = f32[32]{0:T(128)S(1)} all-reduce(f32[32]{0:T(128)S(1)} %reduce_sum.84), channel_id=1, replica_groups=mesh['batch'=16,'patch'=16] {'patch'}, use_global_device_ids=true, to_apply=%region_11.12 | all-reduce | flops 32 | bytes 256 | tf_op jit(solution)/shard_map/psum | solution.py:25
  374.3 3.9 convolution_convert_fusion.1
  378.2 24.3 %all-gather.16.cloned.1.call-done = bf16[1280,1280]{1,0:T(8,128)(2,1)} async-done(((bf16[80,1280]{1,0:T(8,128)(2,1)}), bf16[1280,1280]{1,0:T(8,128)(2,1)}) %all-gather.16.cloned.1.call-update) | async-done | bytes 3276816 | tf_op jit(solution)/shard_map/all_gather | solution.py:84
  402.5 3.8 convolution_convert_fusion
  407.2 87.1 %all-gather.10.cloned.1.call-done = bf16[1280,1280]{1,0:T(8,128)(2,1)} async-done(((bf16[80,1280]{1,0:T(8,128)(2,1)}), bf16[1280,1280]{1,0:T(8,128)(2,1)}) %all-gather.10.cloned.1.call-update) | async-done | bytes 3276816 | tf_op jit(solution)/shard_map/all_gather | solution.py:82
  494.3 3.1 convolution_convert_fusion.2
  497.6 121.3 %all-gather.14.cloned.1.call-done = bf16[2048,1280]{1,0:T(8,128)(2,1)} async-done(((bf16[128,1280]{1,0:T(8,128)(2,1)}), bf16[2048,1280]{1,0:T(8,128)(2,1)}) %all-gather.14.cloned.1.call-update) | async-done | bytes 5242896 | tf_op jit(solution)/shard_map/all_gather | solution.py:90
  618.9 7.9 copy.30
  626.8 114.0 %all-gather.18.cloned.1.call-done = bf16[2048,1280]{1,0:T(8,128)(2,1)} async-done(((bf16[128,1280]{1,0:T(8,128)(2,1)}), bf16[2048,1280]{1,0:T(8,128)(2,1)}) %all-gather.18.cloned.1.call-update) | async-done | bytes 5242896 | tf_op jit(solution)/shard_map/all_gather | solution.py:91
  740.9 8.0 copy.31
  748.8 60.4 %while.10 = (s32[]{:T(128)}, bf16[20,128,64]{1,2,0:T(8,128)(2,1)S(1)}, bf16[20,128,64]{1,2,0:T(8,128)(2,1)S(1)}, bf16[20,2048,64]{1,2,0:T(8,128)(2,1)}, bf16[20,2048,64]{1,2,0:T(8,128)(2,1)}, /*index=5*/s32[]{:T(128)}) while((s32[]{:T(128)}, bf16[20,128,64]{1,2,0:T(8,128)(2,1)S(1)}, bf16[20,128,64]{1,2,0:T(8,128)(2,1)S(1)}, ...), condition=%wide.region_15.16_spmd, body=%wide.region_12.15_spmd.sunk | while | flops 68689664 | bytes 3723845 | solution.py:59
  748.8 1.3 fusion.73
  751.9 1.4 fusion.73
  754.9 1.4 fusion.73
  757.9 1.4 fusion.73
  760.9 1.4 fusion.73
  762.6 1.3 fusion.75
  763.9 1.4 fusion.73
  765.6 1.3 fusion.75
  766.9 1.4 fusion.73
  768.6 1.3 fusion.75
  770.0 1.4 fusion.73
  771.6 1.3 fusion.75
  773.0 1.4 fusion.73
  774.6 1.3 fusion.75
  776.0 1.4 fusion.73
  777.7 1.3 fusion.75
  779.0 1.4 fusion.73
  780.7 1.3 fusion.75
  782.0 1.4 fusion.73
  783.7 1.3 fusion.75
  785.1 1.4 fusion.73
  786.7 1.3 fusion.75
  788.1 1.4 fusion.73
  789.7 1.3 fusion.75
  791.1 1.4 fusion.73
  792.8 1.3 fusion.75
  794.1 1.4 fusion.73
  795.8 1.3 fusion.75
  797.2 1.4 fusion.73
  798.8 1.3 fusion.75
  800.2 1.4 fusion.73
  803.2 1.4 fusion.73
  804.9 1.3 fusion.75
  806.2 1.4 fusion.73
  807.9 1.3 fusion.75
  809.2 20.8 %all-gather.20.cloned.1.call-done = bf16[1280,1280]{1,0:T(8,128)(2,1)} async-done(((bf16[80,1280]{1,0:T(8,128)(2,1)}), bf16[1280,1280]{1,0:T(8,128)(2,1)}) %all-gather.20.cloned.1.call-update) | async-done | bytes 3276816 | tf_op jit(solution)/shard_map/all_gather | solution.py:94
  830.1 3.9 fusion.14
  (106 shorter events, 22.1 us)
Async XLA Ops:
  6.5 206.7 %all-gather.8.cloned.1.call-start = ((), (), s32[]{:S(2)}) async-start(), calls=%async_computation.1 | async-start | bytes 5570560 | tf_op jit(solution)/shard_map/all_gather | solution.py:69
  87.3 287.0 %all-gather.12.cloned.1.call-start = ((), (), s32[]{:S(2)}) async-start(), calls=%async_computation.3 | async-start | bytes 3481600 | tf_op jit(solution)/shard_map/all_gather | solution.py:83
  88.0 314.5 %all-gather.16.cloned.1.call-start = ((), (), s32[]{:S(2)}) async-start(), calls=%async_computation.5 | async-start | bytes 3481600 | tf_op jit(solution)/shard_map/all_gather | solution.py:84
  88.7 405.5 %all-gather.10.cloned.1.call-start = ((), (), s32[]{:S(2)}) async-start(), calls=%async_computation.2 | async-start | bytes 3481600 | tf_op jit(solution)/shard_map/all_gather | solution.py:82
  89.3 155.0 %copy-start.3 = (bf16[3,3,80,1280]{3,2,1,0:T(8,128)(2,1)S(1)}, bf16[3,3,80,1280]{3,2,1,0:T(8,128)(2,1)}, u32[]{:S(2)}) copy-start(bf16[3,3,80,1280]{3,2,1,0:T(8,128)(2,1)} %param.10) | copy-start | bytes 5529604
  89.3 529.6 %all-gather.14.cloned.1.call-start = ((), (), s32[]{:S(2)}) async-start(), calls=%async_computation.4 | async-start | bytes 5570560 | tf_op jit(solution)/shard_map/all_gather | solution.py:90
  244.3 4.4 copy-start.1
  244.3 8.6 %slice-start.8 = ((s8[5242880]{0:T(1024)(128)(4,1)}), s8[4194304]{0:T(1024)(128)(4,1)S(1)}, s32[]{:S(2)}) async-start(s8[5242880]{0:T(1024)(128)(4,1)} %bitcast.122), calls=%async_computation.16 | async-start | bytes 8388608
  248.7 2.5 copy-start
  248.7 4.2 slice-start.9
  251.2 3.5 slice-start
  251.2 5.6 slice-start.6
  252.9 2.2 slice-start.1
  252.9 3.9 slice-start.7
  254.7 3.9 slice-start.4
  256.8 1.8 slice-start.5
  256.9 3.5 slice-start.2
  258.6 1.7 slice-start.3
  260.3 1.7 copy-start.4
  262.0 34.6 %copy-start.2 = (bf16[2,64,1280]{2,1,0:T(8,128)(2,1)S(1)}, bf16[2,64,1280]{2,1,0:T(8,128)(2,1)}, u32[]{:S(2)}) copy-start(bf16[2,64,1280]{2,1,0:T(8,128)(2,1)} %param.9) | copy-start | bytes 983044
  378.2 362.7 %all-gather.18.cloned.1.call-start = ((), (), s32[]{:S(2)}) async-start(), calls=%async_computation.6 | async-start | bytes 5570560 | tf_op jit(solution)/shard_map/all_gather | solution.py:91
  406.4 423.7 %all-gather.20.cloned.1.call-start = ((), (), s32[]{:S(2)}) async-start(), calls=%async_computation.7 | async-start | bytes 3481600 | tf_op jit(solution)/shard_map/all_gather | solution.py:94
Sparse Core Ops, SparseCore 0:
  87.4 125.8 all-gather.7
  215.0 97.4 all-gather.11
  314.3 88.2 all-gather.15
  404.2 90.0 all-gather.9
  495.9 122.9 all-gather.13
  620.6 120.2 all-gather.17
  742.7 87.3 all-gather.19
where the time goes:
time: 850 us; the launch traced here: 841 us
  waiting for transfers between devices  494 us (58%)
  blocking collectives  184 us (22%)
  matrix products  86.5 us (10%)
  local copies, waits for them, and re-layouts  50.5 us (6%)
  between operations  13.9 us (2%)
  other arithmetic  10.9 us (1%)
    all_gather x1, waiting for transfers between devices, on_device(): whole_image = lax.all_gather(activated, 'patch', axis=0, tiled=True)  124 us
    all_gather x1, waiting for transfers between devices, on_device(): lax.all_gather(key_local, 'patch', axis=0, tiled=True)  121 us
    all_gather x1, waiting for transfers between devices, on_device(): lax.all_gather(value_local, 'patch', axis=0, tiled=True)  114 us
    all_gather x1, waiting for transfers between devices, on_device(): lax.all_gather(w_query, 'patch', axis=0, tiled=True)  87.1 us
    psum x2, blocking collectives, group_norm(): lax.psum(jnp.sum(jnp.square(deviation), axis=(0, 2)), 'patch') / entries  78.2 us
    psum x2, blocking collectives, group_norm(): centre = lax.psum(jnp.sum(grouped, axis=(0, 2)), 'patch') / entries  74.2 us
    dot_general x13, matrix products, contract(): lax.dot_general(left, right, (((1,), (1,)), ((), ())), preferred_element_...  32.6 us
    all_to_all x1, blocking collectives, on_device(): lax.all_to_all(convolved.astype(jnp.bfloat16), 'patch', split_axis=0, con...  31.8 us
  transfers between devices with their start and end apart: 7, of which 6 were waited for; matrix products, arithmetic and copies ran while one was open for 16% of the time, Pallas kernels for 0%

commit v1 on v0

v1 whole, which is shorter than its diff:
```python
import jax
import jax.numpy as jnp
from jax import lax
from jax.experimental import pallas as pl
from jax.experimental.pallas import tpu as pltpu
from jax.sharding import PartitionSpec as P

C = 1280
HEADS = 20
HEAD_DIM = 64
GROUPS = 32
GROUP = C // GROUPS
NY, NZ = 4, 4
BLK = 128
ROWS_Y = 512
CB = C // 16
CZ = C // 4
EPS = 1e-05
MESH = pl.DeviceIdType.MESH
F32 = jnp.float32
BF16 = jnp.bfloat16


def dot_nt(left, right):
    return lax.dot_general(left, right, (((1,), (1,)), ((), ())), preferred_element_type=F32)


def dot_nn(left, right):
    return lax.dot_general(left, right, (((1,), (0,)), ((), ())), preferred_element_type=F32)


def kernel(
    lat_in, cw_in, bias_in, wq_in, wk_in, wv_in, wo_in, out_ref,
    lat, act, cw, wown, wqkv, wo, st1s, st1, st2s, st2, gmat, gmat_t, sel,
    gn1, gn2, ubuf, hidg, nrm, hnat, qb, kv, att, attg,
    s_loc, s_st1, r_st1, s_lat, r_lat, s_halo, r_halo, s_cw, r_cw, s_cws, r_cws,
    s_qw, r_qw, s_qws, r_qws, l_qw, s_woz, r_woz, s_woy, r_woy, s_wos, r_wos,
    s_st2, r_st2, s_hid, r_hid, s_kv, r_kv, s_att, r_att,
):
    p = lax.axis_index("patch")
    b = lax.axis_index("batch")
    y = p // 4
    z = p % 4
    c = b % 2
    sib = b + 1 - 2 * c
    up = (y + 1) % 4
    down = (y + 3) % 4
    opposite = (y + 2) % 4
    half = pl.ds(pl.multiple_of(c * (C // 2), 128), C // 2)
    other = pl.ds(pl.multiple_of((1 - c) * (C // 2), 128), C // 2)
    pending = []

    def patch(yy, zz):
        return {"batch": b, "patch": 4 * yy + zz}

    sibling = {"batch": sib, "patch": p}

    def remote(src, dst, ssem, rsem, dev):
        return pltpu.make_async_remote_copy(
            src_ref=src, dst_ref=dst, send_sem=ssem, recv_sem=rsem, device_id=dev, device_id_type=MESH
        )

    def when(cond, f):
        if cond is None:
            f()
        else:
            pl.when(cond)(f)

    def send(make, cond=None):
        when(cond, lambda: make().start())
        pending.append((cond, make))

    own_rows = pl.ds(pl.multiple_of(64 + BLK * z, 64), BLK)
    loc = [
        pltpu.make_async_copy(lat_in, lat.at[own_rows], s_loc.at[0]),
        pltpu.make_async_copy(cw_in, cw.at[:, :, y], s_loc.at[1]),
        pltpu.make_async_copy(wq_in, wown.at[0], s_loc.at[2]),
        pltpu.make_async_copy(wk_in, wown.at[1], s_loc.at[3]),
        pltpu.make_async_copy(wv_in, wown.at[2], s_loc.at[4]),
        pltpu.make_async_copy(wo_in, wown.at[3], s_loc.at[5]),
        pltpu.make_async_copy(wo_in.at[:, half], wo.at[p, :, half], s_loc.at[6]),
    ]
    for copy in loc:
        copy.start()
    barrier = pltpu.get_barrier_semaphore()
    for d in range(1, 16):
        pl.semaphore_signal(
            barrier, inc=1, device_id={"batch": b, "patch": (p + d) % 16}, device_id_type=MESH
        )
    pl.semaphore_signal(barrier, inc=1, device_id=sibling, device_id_type=MESH)

    st1s[...] = jnp.zeros_like(st1s)
    loc[0].wait()
    mine = lat[own_rows].astype(F32)
    mean = jnp.sum(mine, axis=0, keepdims=True) * (1.0 / BLK)
    m2 = jnp.sum(jnp.square(mine - mean), axis=0, keepdims=True)
    for j in range(10):
        st1s[j : j + 1, :] = mean[:, 128 * j : 128 * j + 128]
        st1s[16 + j : 17 + j, :] = m2[:, 128 * j : 128 * j + 128]
    st1s[15:16, 0:CB] = bias_in[...]

    pl.semaphore_wait(barrier, 16)

    for d in range(1, 16):
        send(
            lambda d=d: remote(
                st1s, st1.at[p], s_st1.at[d], r_st1.at[d], {"batch": b, "patch": (p + d) % 16}
            )
        )
    st1[p] = st1s[...]

    def lat_rows(k):
        return lat.at[pl.ds(pl.multiple_of(64 + BLK * k, 64), BLK)]

    def lat_copy(k, way):
        zz = z + 1 if way == 0 else z - 1
        return remote(lat_rows(k), lat_rows(k), s_lat.at[way, k], r_lat.at[k], patch(y, zz))

    send(lambda: lat_copy(z, 0), z < 3)
    send(lambda: lat_copy(z, 1), z > 0)

    loc[1].wait()

    def cw_copy(src_y, to_y, slot):
        ref = cw.at[:, :, src_y, :, half]
        return remote(ref, ref, s_cw.at[slot], r_cw.at[slot], patch(to_y, z))

    def cw_forward(src_y, slot):
        ref = cw.at[:, :, src_y, :, half]
        return remote(ref, ref, s_cws.at[slot], r_cws.at[slot], sibling)

    def cw_arrival(src_y, slot):
        ref = cw.at[:, :, src_y, :, other]
        return remote(ref, ref, s_cws.at[slot], r_cws.at[slot], sibling)

    send(lambda: cw_copy(y, up, 0))
    send(lambda: cw_copy(y, down, 1))

    gi = lax.broadcasted_iota(jnp.int32, (C, 128), 0) - GROUP * lax.broadcasted_iota(jnp.int32, (C, 128), 1)
    gmat[...] = jnp.where((gi >= 0) & (gi < GROUP), 1.0, 0.0).astype(BF16)
    ti = lax.broadcasted_iota(jnp.int32, (128, C), 1) - GROUP * lax.broadcasted_iota(jnp.int32, (128, C), 0)
    gmat_t[...] = jnp.where((ti >= 0) & (ti < GROUP), 1.0, 0.0).astype(BF16)
    for yy in range(4):
        rows = lax.broadcasted_iota(jnp.int32, (CZ, CZ), 0) - CB * z
        cols = lax.broadcasted_iota(jnp.int32, (CZ, CZ), 1) - CB * yy
        hit = (rows == cols) & (cols >= 0) & (cols < CB)
        sel[CZ * yy : CZ * yy + CZ, :] = jnp.where(hit, 1.0, 0.0).astype(BF16)

    def split_rows(x):
        hi = x.astype(BF16).astype(F32)
        mid = (x - hi).astype(BF16).astype(F32)
        return jnp.concatenate([hi, mid, x - hi - mid], axis=0).astype(BF16)

    def join_rows(x):
        return x[0:8] + x[8:16] + x[16:24]

    def group_sums(x):
        n = x.shape[1]
        sums = join_rows(dot_nn(split_rows(x), gmat[0:n, :]))
        return join_rows(dot_nn(split_rows(sums), gmat_t[:, 0:n]))

    for d in range(1, 16):
        q = (p + 16 - d) % 16
        remote(st1s, st1.at[q], s_st1.at[d], r_st1.at[d], {"batch": b, "patch": q}).wait_recv()
    means = st1[:, 0:16, :]
    mean_c = jnp.sum(means, axis=0) * (1.0 / 16)
    m2_c = jnp.sum(st1[:, 16:32, :], axis=0) + BLK * jnp.sum(jnp.square(means - mean_c[None]), axis=0)

    def to_lanes(x, n):
        full = jnp.concatenate([x[j : j + 1, :] for j in range(n)], axis=1)
        return full

    mean_l = jnp.broadcast_to(to_lanes(mean_c, 10), (8, C))
    m2_l = jnp.broadcast_to(to_lanes(m2_c, 10), (8, C))
    centre = group_sums(mean_l) * (1.0 / GROUP)
    spread = group_sums(m2_l + 2048.0 * jnp.square(mean_l - centre)) * (1.0 / (2048 * GROUP))
    gn1[0] = centre
    gn1[1] = lax.rsqrt(spread + EPS)

    def activate(start, count):
        def body(i, carry):
            rows = pl.ds(pl.multiple_of(start + 16 * i, 16), 16)
            v = lat[rows].astype(F32)
            v = (v - gn1[0, 0:1, :]) * gn1[1, 0:1, :]
            act[rows] = (v / (1.0 + jnp.exp(-v))).astype(BF16)
            return carry

        lax.fori_loop(0, count // 16, body, 0)

    activate(64 + BLK * z, BLK)

    def halo_up():
        return remote(
            lat.at[pl.ds(512, 64)], lat.at[pl.ds(0, 64)], s_halo.at[0], r_halo.at[0], patch(y + 1, z)
        )

    def halo_down():
        return remote(
            lat.at[pl.ds(64, 64)], lat.at[pl.ds(576, 64)], s_halo.at[1], r_halo.at[1], patch(y - 1, z)
        )

    send(halo_up, (z == 3) & (y < 3))
    send(halo_down, (z == 0) & (y > 0))
    for k in range(1, 4):
        def below(k=k):
            lat_copy(z - k, 0).wait_recv()

        def above(k=k):
            lat_copy(z + k, 1).wait_recv()

        when(z - k >= 0, below)
        send(lambda k=k: lat_copy(z - k, 0), (z - k >= 0) & (z < 3))
        when(z + k <= 3, above)
        send(lambda k=k: lat_copy(z + k, 1), (z + k <= 3) & (z > 0))
        send(halo_up, (z + k == 3) & (y < 3))
        send(halo_down, (z - k == 0) & (y > 0))
        when(z - k >= 0, lambda k=k: activate(64 + BLK * (z - k), BLK))
        when(z + k <= 3, lambda k=k: activate(64 + BLK * (z + k), BLK))

    cw_copy(down, y, 0).wait_recv()
    send(lambda: cw_copy(down, up, 2), c == 0)
    send(lambda: cw_forward(down, 0))
    cw_copy(up, y, 1).wait_recv()
    send(lambda: cw_copy(up, down, 2), c == 1)
    send(lambda: cw_forward(up, 1))

    for copy in loc[2:]:
        copy.wait()

    def qw_rows(k):
        return pl.ds(pl.multiple_of(CB * k, 16), CB)

    def qw_copy(yy, k, zz):
        return remote(
            wown.at[0:3, :, half], wqkv.at[:, qw_rows(k), half], s_qw.at[yy], r_qw.at[k], patch(yy, zz)
        )

    def qw_local():
        return pltpu.make_async_copy(wown.at[0:3, :, half], wqkv.at[:, qw_rows(z), half], l_qw.at[0])

    for yy in range(4):
        send(lambda yy=yy: qw_copy(yy, z, y), (y != yy) | (z != y))
    when(z == y, lambda: qw_local().start())

    when(y > 0, lambda: halo_up().wait_recv())
    when(y > 0, lambda: activate(0, 64))
    when(y < 3, lambda: halo_down().wait_recv())
    when(y < 3, lambda: activate(576, 64))

    def zero_top():
        act[0:64] = jnp.zeros((64, C), BF16)

    def zero_bottom():
        act[576:640] = jnp.zeros((64, C), BF16)

    when(y == 0, zero_top)
    when(y == 3, zero_bottom)

    cw_copy(opposite, y, 2).wait_recv()
    send(lambda: cw_forward(opposite, 2))
    cw_arrival(down, 0).wait_recv()
    cw_arrival(up, 1).wait_recv()
    cw_arrival(opposite, 2).wait_recv()

    bias = jnp.concatenate([st1[4 * yy + z, 15:16, 0:CB] for yy in range(4)], axis=1)
    CHUNK = 256

    def conv_chunk(j, carry):
        total = jnp.zeros((CHUNK, 3 * CZ), F32)
        for dr in range(3):
            rows = pl.ds(pl.multiple_of(CHUNK * j + 64 * dr, 64), CHUNK)
            total = total + dot_nt(act[rows], cw[dr].reshape(3 * CZ, C))
        ubuf[...] = total
        column = lax.broadcasted_iota(jnp.int32, (CHUNK, CZ), 0) % 64
        left = pltpu.roll(ubuf[:, 0:CZ], 1, 0)
        right = pltpu.roll(ubuf[:, 2 * CZ : 3 * CZ], CHUNK - 1, 0)
        value = ubuf[:, CZ : 2 * CZ]
        value = value + jnp.where(column == 0, 0.0, left) + jnp.where(column == 63, 0.0, right)
        own = lat[pl.ds(pl.multiple_of(64 + CHUNK * j, 64), CHUNK)]
        value = value + dot_nn(own, sel[...]) + bias
        hidg[z, pl.ds(pl.multiple_of(CHUNK * j, 128), CHUNK), :] = value.astype(BF16)
        return carry

    lax.fori_loop(0, ROWS_Y // CHUNK, conv_chunk, 0)

    def hid_copy(k, way):
        zz = z + 1 if way == 0 else z - 1
        return remote(hidg.at[k], hidg.at[k], s_hid.at[way, k], r_hid.at[k], patch(y, zz))

    send(lambda: hid_copy(z, 0), z < 3)
    send(lambda: hid_copy(z, 1), z > 0)

    st2s[...] = jnp.zeros_like(st2s)
    hidden = hidg[z].astype(F32)
    mean = jnp.sum(hidden, axis=0, keepdims=True) * (1.0 / ROWS_Y)
    m2 = jnp.sum(jnp.square(hidden - mean), axis=0, keepdims=True)
    for j in range(3):
        width = min(128, CZ - 128 * j)
        st2s[j : j + 1, 0:width] = mean[:, 128 * j : 128 * j + width]
        st2s[4 + j : 5 + j, 0:width] = m2[:, 128 * j : 128 * j + width]
    for d in range(1, 16):
        send(
            lambda d=d: remote(
                st2s, st2.at[p], s_st2.at[d], r_st2.at[d], {"batch": b, "patch": (p + d) % 16}
            )
        )
    st2[p] = st2s[...]

    def qw_forward(k):
        ref = wqkv.at[:, qw_rows(k), half]
        return remote(ref, ref, s_qws.at[k], r_qws.at[k], sibling)

    def qw_arrival(k):
        ref = wqkv.at[:, qw_rows(k), other]
        return remote(ref, ref, s_qws.at[k], r_qws.at[k], sibling)

    for k in range(4):
        remote_wait = (y != z) | (z != k)
        when(remote_wait, lambda k=k: qw_copy(0, k, 0).wait_recv())
        when(~remote_wait, lambda: qw_local().wait())
        send(lambda k=k: qw_forward(k))

    for d in range(1, 16):
        q = (p + 16 - d) % 16
        remote(st2s, st2.at[q], s_st2.at[d], r_st2.at[d], {"batch": b, "patch": q}).wait_recv()
    parts = [[st2[4 * yy + zz] for zz in range(4)] for yy in range(4)]
    mean_rows, m2_rows = [], []
    for zz in range(4):
        col = [parts[yy][zz] for yy in range(4)]
        m = (col[0] + col[1] + col[2] + col[3]) * 0.25
        dev = sum(jnp.square(x - m) for x in col)
        total = col[0] + col[1] + col[2] + col[3]
        m2_all = total[4:8] + ROWS_Y * dev[0:4]
        mean_rows.append(to_lanes(m, 3)[:, 0:CZ])
        m2_rows.append(to_lanes(m2_all, 3)[:, 0:CZ])
    mean_l = jnp.concatenate(mean_rows + mean_rows, axis=0)
    m2_l = jnp.concatenate(m2_rows + m2_rows, axis=0)
    centre = group_sums(mean_l) * (1.0 / GROUP)
    spread = group_sums(m2_l + 2048.0 * jnp.square(mean_l - centre)) * (1.0 / (2048 * GROUP))
    gn2[0] = centre
    gn2[1] = lax.rsqrt(spread + EPS)

    for k in range(1, 4):
        when(z - k >= 0, lambda k=k: hid_copy(z - k, 0).wait_recv())
        send(lambda k=k: hid_copy(z - k, 0), (z - k >= 0) & (z < 3))
        when(z + k <= 3, lambda k=k: hid_copy(z + k, 1).wait_recv())
        send(lambda k=k: hid_copy(z + k, 1), (z + k <= 3) & (z > 0))

    def wo_z(k, way):
        zz = z + 1 if way == 0 else z - 1
        ref = wo.at[4 * y + k, :, half]
        return remote(ref, ref, s_woz.at[way, k], r_woz.at[k], patch(y, zz))

    send(lambda: wo_z(z, 0), z < 3)
    send(lambda: wo_z(z, 1), z > 0)

    def normalize(i, carry):
        rows = pl.ds(pl.multiple_of(16 * i, 16), 16)
        blocks = [
            (hidg[zz, rows, :].astype(F32) - gn2[0, zz : zz + 1, :]) * gn2[1, zz : zz + 1, :]
            for zz in range(4)
        ]
        nrm[rows] = jnp.concatenate(
            [blocks[zz][:, CB * yy : CB * yy + CB] for yy in range(4) for zz in range(4)], axis=1
        ).astype(BF16)
        return carry

    lax.fori_loop(0, ROWS_Y // 16, normalize, 0)

    for k in range(4):
        qw_arrival(k).wait_recv()

    def project(j, carry):
        rows = pl.ds(pl.multiple_of(256 * j, 256), 256)
        block = nrm[rows]
        kv[0, y, rows, :] = dot_nt(block, wqkv[1]).astype(BF16)
        kv[1, y, rows, :] = dot_nt(block, wqkv[2]).astype(BF16)
        qb[rows] = (dot_nt(block, wqkv[0]).astype(BF16).astype(F32) * HEAD_DIM**-0.5).astype(BF16)
        return carry

    lax.fori_loop(0, ROWS_Y // 256, project, 0)

    def kv_copy(which, src_y, to_y, slot):
        ref = kv.at[which, src_y]
        return remote(ref, ref, s_kv.at[which, slot], r_kv.at[which, slot], patch(to_y, z))

    for which in range(2):
        send(lambda which=which: kv_copy(which, y, up, 0))
        send(lambda which=which: kv_copy(which, y, down, 1))

    def residual(i, carry):
        rows = pl.ds(pl.multiple_of(BLK * z + 16 * i, 16), 16)
        blocks = [hidg[zz, rows, :].astype(F32) for zz in range(4)]
        hnat[pl.ds(pl.multiple_of(16 * i, 16), 16)] = jnp.concatenate(
            [blocks[zz][:, CB * yy : CB * yy + CB] for yy in range(4) for zz in range(4)], axis=1
        )
        return carry

    lax.fori_loop(0, BLK // 16, residual, 0)

    for k in range(1, 4):
        when(z - k >= 0, lambda k=k: wo_z(z - k, 0).wait_recv())
        send(lambda k=k: wo_z(z - k, 0), (z - k >= 0) & (z < 3))
        when(z + k <= 3, lambda k=k: wo_z(z + k, 1).wait_recv())
        send(lambda k=k: wo_z(z + k, 1), (z + k <= 3) & (z > 0))

    kv_copy(0, down, y, 0).wait_recv()
    send(lambda: kv_copy(0, down, up, 2))
    kv_copy(1, up, y, 1).wait_recv()
    send(lambda: kv_copy(1, up, down, 2))

    def wo_row(src_y, mask):
        return wo.at[pl.ds(4 * src_y, 4), :, mask]

    def wo_y(src_y, to_y, slot):
        ref = wo_row(src_y, half)
        return remote(ref, ref, s_woy.at[slot], r_woy.at[slot], patch(to_y, z))

    send(lambda: wo_y(y, up, 0))
    send(lambda: wo_y(y, down, 1))
    kv_copy(1, down, y, 0).wait_recv()
    kv_copy(0, up, y, 1).wait_recv()
    kv_copy(0, opposite, y, 2).wait_recv()
    kv_copy(1, opposite, y, 2).wait_recv()

    def att_copy(j):
        return remote(att.at[j], attg.at[z], s_att.at[j], r_att.at[z], patch(y, j))

    def att_from(k):
        return remote(att.at[k], attg.at[k], s_att.at[k], r_att.at[k], patch(y, k))

    def attend(j):
        rows = pl.ds(pl.multiple_of(BLK * j, 128), BLK)
        for pair in range(3):
            width = min(128, CZ - 128 * pair)
            lanes = slice(128 * pair, 128 * pair + width)
            query = qb[rows, lanes]
            keys = kv[0, :, :, lanes].reshape(2048, width)
            values = kv[1, :, :, lanes].reshape(2048, width)
            lane = lax.broadcasted_iota(jnp.int32, (BLK, width), 1)
            result = None
            for side in range(width // 64):
                q1 = query
                if width > 64:
                    keep = (lane >= 64 * side) & (lane < 64 * side + 64)
                    q1 = jnp.where(keep, query.astype(F32), 0.0).astype(BF16)
                scores = dot_nt(q1, keys)
                peak = jnp.max(scores, axis=1, keepdims=True)
                unnormalized = jnp.exp(scores - peak)
                row_total = jnp.sum(unnormalized, axis=1, keepdims=True)
                mix = dot_nn(unnormalized.astype(BF16), values) / row_total
                result = mix if result is None else jnp.where(lane < 64, result, mix)
            att[j, :, lanes] = result.astype(BF16)

    def attend_step(t, carry):
        j = (z + 1 + t) % 4
        attend(j)
        pl.when(t < 3)(lambda: att_copy(j).start())
        return carry

    lax.fori_loop(0, 4, attend_step, 0)
    attg[z] = att[z]
    for k in range(4):
        pending.append((z != k, lambda k=k: att_copy(k)))

    wo_y(down, y, 0).wait_recv()
    send(lambda: wo_y(down, up, 2), c == 0)
    wo_y(up, y, 1).wait_recv()
    send(lambda: wo_y(up, down, 2), c == 1)
    wo_y(opposite, y, 2).wait_recv()

    def wo_forward(k):
        ref = wo_row(k, half)
        return remote(ref, ref, s_wos.at[k], r_wos.at[k], sibling)

    def wo_arrival(k):
        ref = wo_row(k, other)
        return remote(ref, ref, s_wos.at[k], r_wos.at[k], sibling)

    for k in range(4):
        send(lambda k=k: wo_forward(k))
    for k in range(4):
        wo_arrival(k).wait_recv()
    for k in range(4):
        when(z != k, lambda k=k: att_from(k).wait_recv())

    whole = jnp.concatenate([attg[k].astype(F32) for k in range(4)], axis=1).astype(BF16)
    out_ref[...] = (hnat[...] + dot_nt(whole, wo[...].reshape(C, C))).astype(BF16)

    for cond, make in pending:
        when(cond, lambda make=make: make().wait_send())


def on_device(latent, conv_weight, channel_bias, w_query, w_key, w_value, w_out):
    any_space = pl.BlockSpec(memory_space=pl.ANY)
    vmem = pl.BlockSpec(memory_space=pltpu.VMEM)
    dma = pltpu.SemaphoreType.DMA
    out = pl.pallas_call(
        kernel,
        out_shape=jax.ShapeDtypeStruct((BLK, C), BF16),
        in_specs=[any_space, any_space, vmem, any_space, any_space, any_space, any_space],
        out_specs=vmem,
        scratch_shapes=[
            pltpu.VMEM((640, C), BF16),
            pltpu.VMEM((640, C), BF16),
            pltpu.VMEM((3, 3, 4, CB, C), BF16),
            pltpu.VMEM((4, CB, C), BF16),
            pltpu.VMEM((3, CZ, C), BF16),
            pltpu.VMEM((16, CB, C), BF16),
            pltpu.VMEM((32, 128), F32),
            pltpu.VMEM((16, 32, 128), F32),
            pltpu.VMEM((8, 128), F32),
            pltpu.VMEM((16, 8, 128), F32),
            pltpu.VMEM((C, 128), BF16),
            pltpu.VMEM((128, C), BF16),
            pltpu.VMEM((C, CZ), BF16),
            pltpu.VMEM((2, 8, C), F32),
            pltpu.VMEM((2, 8, CZ), F32),
            pltpu.VMEM((256, 3 * CZ), F32),
            pltpu.VMEM((4, ROWS_Y, CZ), BF16),
            pltpu.VMEM((ROWS_Y, C), BF16),
            pltpu.VMEM((BLK, C), F32),
            pltpu.VMEM((ROWS_Y, CZ), BF16),
            pltpu.VMEM((2, 4, ROWS_Y, CZ), BF16),
            pltpu.VMEM((4, BLK, CZ), BF16),
            pltpu.VMEM((4, BLK, CZ), BF16),
            dma((7,)), dma((16,)), dma((16,)), dma((2, 4)), dma((4,)), dma((2,)), dma((2,)),
            dma((3,)), dma((3,)), dma((3,)), dma((3,)),
            dma((4,)), dma((4,)), dma((4,)), dma((4,)), dma((1,)),
            dma((2, 4)), dma((4,)), dma((3,)), dma((3,)), dma((4,)), dma((4,)),
            dma((16,)), dma((16,)), dma((2, 4)), dma((4,)), dma((2, 3)), dma((2, 3)), dma((4,)), dma((4,)),
        ],
        compiler_params=pltpu.CompilerParams(
            collective_id=0, has_side_effects=True, vmem_limit_bytes=60 * 1024 * 1024
        ),
    )(
        latent.reshape(BLK, C), conv_weight, channel_bias.reshape(1, CB), w_query, w_key, w_value, w_out
    )
    return out.reshape(latent.shape)


def solution(mesh):
    return jax.shard_map(
        on_device,
        mesh=mesh,
        in_specs=(
            P(("batch", "patch"), None, None),
            P(None, None, "patch", None),
            P("patch"),
            P("patch", None),
            P("patch", None),
            P("patch", None),
            P("patch", None),
        ),
        out_specs=P(("batch", "patch"), None, None),
        check_vma=False,
    )
```

time: 850 us -> 222 us (0.26)
  waiting for transfers between devices: 494 us -> 0 us
  Pallas kernels: 0 us -> 218 us
  blocking collectives: 184 us -> 0 us
  matrix products: 86.5 us -> 0 us
  local copies, waits for them, and re-layouts: 50.5 us -> 1.72 us
  between operations: 13.9 us -> 0.01 us
  other arithmetic: 10.9 us -> 0 us
    all_gather x7 -> x0, waiting for transfers between devices: 492 us -> none  [the longest x1 124 us: on_device(): whole_image = lax.all_gather(activated, 'patch', axis=0, tiled=True)]
    pallas_call x0 -> x1, Pallas kernels: none -> 218 us  [on_device(): pl.pallas_call(kernel, out_shape=jax.ShapeDtypeStruct((BLK, C), BF16), in...]
    psum x4 -> x0, blocking collectives: 152 us -> none  [the longest x2 78.2 us: group_norm(): lax.psum(jnp.sum(jnp.square(deviation), axis=(0, 2)), 'patch') / entries]
    dot_general x53 -> x0, matrix products: 86.5 us -> none  [the longest x13 32.6 us: contract(): lax.dot_general(left, right, (((1,), (1,)), ((), ())), preferred_element_...]
    all_to_all x1 -> x0, blocking collectives: 31.8 us -> none  [on_device(): lax.all_to_all(convolved.astype(jnp.bfloat16), 'patch', split_axis=0, con...]
    slice x1 -> x0, local copies, waits for them, and re-layouts: 31 us -> none  [convolve(): padded[row_shift:row_shift + row_count, col_shift:col_shift + columns, :]]
    all_gather x2 -> x0, local copies, waits for them, and re-layouts: 15.9 us -> none  [the longest x1 7.97 us: on_device(): lax.all_gather(value_local, 'patch', axis=0, tiled=True)]
    reduce_sum x28 -> x0, other arithmetic: 8.81 us -> none  [the longest x20 6.08 us: one_head(): row_total = jnp.sum(unnormalized, axis=1, keepdims=True)]
  transfers between devices with their start and end apart: 7 -> 0, of which waited for: 6 -> 0; matrix products, arithmetic and copies ran while one was open for 16% -> 0% of each run, Pallas kernels for 0% -> 0%
where the time goes in v1:
time: 222 us; the launch traced here: 220 us
  Pallas kernels  218 us (98%)
    pallas_call x1, Pallas kernels, on_device(): pl.pallas_call(kernel, out_shape=jax.ShapeDtypeStruct((BLK, C), BF16), in...  218 us

profile of v1, /device:TPU:8, one launch (start us, length us, event | category | flops | bytes accessed | tf_op | source)
XLA Modules:
  0.0 219.7 jit_solution(11582654902901659859)
XLA Ops:
  0.0 217.9 %shard_map.73 = bf16[128,1280]{1,0:T(8,128)(2,1)} custom-call(bf16[128,1280]{1,0:T(8,128)(2,1)} %bitcast.4, bf16[3,3,80,1280]{3,2,1,0:T(8,128)(2,1)} %cw_in.1, f32[1,80]{1,0:T(1,128)} %bitcast.5, bf16[80,1280]{1,0:T(8,128)(2,1)} %wq_in.1, bf16[80,1280]{1,0:T(8,128)(2,1)} %wk_in.1, bf16[80,1280]{1,0:T(8,128)(2,1)} %wv_in.1, bf16[80,1280]{1,0:T(8,128)(2,1)} %wo_in.1), custom_call_target="tpu_custom_call" | custom-call | tf_op jit(solution)/shard_map/pallas_call | solution.py:498
  218.0 1.7 copy.9

commit v2 on v1

--- a/solution.py
+++ b/solution.py
@@ -34,7 +34,8 @@
     lat, act, cw, wown, wqkv, wo, st1s, st1, st2s, st2, gmat, gmat_t, sel,
     gn1, gn2, ubuf, hidg, nrm, hnat, qb, kv, att, attg,
     s_loc, s_st1, r_st1, s_lat, r_lat, s_halo, r_halo, s_cw, r_cw, s_cws, r_cws,
-    s_qw, r_qw, s_qws, r_qws, l_qw, s_woz, r_woz, s_woy, r_woy, s_wos, r_wos,
+    s_ct, r_ct, s_cx, r_cx, s_cts, r_cts,
+    s_qa, r_qa, l_qa, s_qb, r_qb, s_qc, r_qc, s_qd, r_qd, s_woz, r_woz, s_woy, r_woy, s_wos, r_wos,
     s_st2, r_st2, s_hid, r_hid, s_kv, r_kv, s_att, r_att,
 ):
     p = lax.axis_index("patch")
@@ -42,6 +43,7 @@
     y = p // 4
     z = p % 4
     c = b % 2
+    x = (b // 2) % 4
     sib = b + 1 - 2 * c
     up = (y + 1) % 4
     down = (y + 3) % 4
@@ -53,6 +55,9 @@
     def patch(yy, zz):
         return {"batch": b, "patch": 4 * yy + zz}
 
+    def across(d):
+        return {"batch": b - 2 * x + 2 * ((x + d) % 4), "patch": p}
+
     sibling = {"batch": sib, "patch": p}
 
     def remote(src, dst, ssem, rsem, dev):
@@ -73,7 +78,7 @@
     own_rows = pl.ds(pl.multiple_of(64 + BLK * z, 64), BLK)
     loc = [
         pltpu.make_async_copy(lat_in, lat.at[own_rows], s_loc.at[0]),
-        pltpu.make_async_copy(cw_in, cw.at[:, :, y], s_loc.at[1]),
+        pltpu.make_async_copy(cw_in, cw.at[:, y], s_loc.at[1]),
         pltpu.make_async_copy(wq_in, wown.at[0], s_loc.at[2]),
         pltpu.make_async_copy(wk_in, wown.at[1], s_loc.at[3]),
         pltpu.make_async_copy(wv_in, wown.at[2], s_loc.at[4]),
@@ -88,6 +93,8 @@
             barrier, inc=1, device_id={"batch": b, "patch": (p + d) % 16}, device_id_type=MESH
         )
     pl.semaphore_signal(barrier, inc=1, device_id=sibling, device_id_type=MESH)
+    for d in range(1, 4):
+        pl.semaphore_signal(barrier, inc=1, device_id=across(d), device_id_type=MESH)
 
     st1s[...] = jnp.zeros_like(st1s)
     loc[0].wait()
@@ -99,7 +106,7 @@
         st1s[16 + j : 17 + j, :] = m2[:, 128 * j : 128 * j + 128]
     st1s[15:16, 0:CB] = bias_in[...]
 
-    pl.semaphore_wait(barrier, 16)
+    pl.semaphore_wait(barrier, 19)
 
     for d in range(1, 16):
         send(
@@ -120,21 +127,112 @@
     send(lambda: lat_copy(z, 1), z > 0)
 
     loc[1].wait()
+    around = (down, up, opposite)
+
+    def cw_ref(src_y, mask):
+        return cw.at[0:5, src_y, :, mask]
 
     def cw_copy(src_y, to_y, slot):
-        ref = cw.at[:, :, src_y, :, half]
+        ref = cw_ref(src_y, half)
         return remote(ref, ref, s_cw.at[slot], r_cw.at[slot], patch(to_y, z))
 
-    def cw_forward(src_y, slot):
-        ref = cw.at[:, :, src_y, :, half]
-        return remote(ref, ref, s_cws.at[slot], r_cws.at[slot], sibling)
-
-    def cw_arrival(src_y, slot):
-        ref = cw.at[:, :, src_y, :, other]
-        return remote(ref, ref, s_cws.at[slot], r_cws.at[slot], sibling)
-
+    def cw_other(r, mask):
+        ref = cw_ref(around[r], mask)
+        return remote(ref, ref, s_cws.at[r], r_cws.at[r], sibling)
+
+    def ct_copy(src_y, to_y, slot):
+        ref = cw.at[5 + x, src_y, :, half]
+        return remote(ref, ref, s_ct.at[slot], r_ct.at[slot], patch(to_y, z))
+
+    def cx_copy(r, d):
+        ref = cw.at[5 + x, around[r], :, half]
+        return remote(ref, ref, s_cx.at[r, d], r_cx.at[r, d], across(d))
+
+    def cx_from(r, d):
+        ref = cw.at[5 + (x + 4 - d) % 4, around[r], :, half]
+        return remote(ref, ref, s_cx.at[r, d], r_cx.at[r, d], across(d))
+
+    def ct_other(r, mask):
+        ref = cw.at[5:9, around[r], :, mask]
+        return remote(ref, ref, s_cts.at[r], r_cts.at[r], sibling)
+
+    send(lambda: ct_copy(y, up, 0))
+    send(lambda: ct_copy(y, down, 1))
+
+    for copy in loc[2:]:
+        copy.wait()
+    carrier = x < 3
+    diagonal = y == z
+    turn = (y - z + 4) % 4
+
+    def qa_rows(k):
+        return wqkv.at[x, pl.ds(pl.multiple_of(CB * k, 16), CB), half]
+
+    def qa_copy(k):
+        return remote(wown.at[x, :, half], qa_rows(k), s_qa.at[0], r_qa.at[k], patch(y, y))
+
+    def qa_local():
+        return pltpu.make_async_copy(wown.at[x, :, half], qa_rows(z), l_qa.at[0])
+
+    def qb_copy(to_y, slot):
+        ref = wqkv.at[x, :, half]
+        return remote(ref, ref, s_qb.at[slot], r_qb.at[0], patch(to_y, z))
+
+    def qc_copy(d):
+        ref = wqkv.at[x, :, half]
+        return remote(ref, ref, s_qc.at[d], r_qc.at[d], across(d))
+
+    def qc_from(d):
+        ref = wqkv.at[(x + 4 - d) % 4, :, half]
+        return remote(ref, ref, s_qc.at[d], r_qc.at[d], across(d))
+
+    def qd_other(m, mask):
+        ref = wqkv.at[m, :, mask]
+        return remote(ref, ref, s_qd.at[m], r_qd.at[m], sibling)
+
+    def spread_q(cond):
+        for d in range(1, 4):
+            send(lambda d=d: qc_copy(d), carrier & cond)
+
+    send(lambda: qa_copy(z), carrier & (z != y))
+    when(carrier & diagonal, lambda: qa_local().start())
     send(lambda: cw_copy(y, up, 0))
     send(lambda: cw_copy(y, down, 1))
+
+    def service_1():
+        ct_copy(down, y, 0).wait_recv()
+        send(lambda: ct_copy(down, up, 2), c == 0)
+        ct_copy(up, y, 1).wait_recv()
+        send(lambda: ct_copy(up, down, 2), c == 1)
+        for r in range(2):
+            for d in range(1, 4):
+                send(lambda r=r, d=d: cx_copy(r, d))
+        for k in range(4):
+            when(carrier & diagonal & (z != k), lambda k=k: qa_copy(k).wait_recv())
+        when(carrier & diagonal, lambda: qa_local().wait())
+        send(lambda: qb_copy(up, 0), carrier & diagonal)
+        send(lambda: qb_copy(down, 1), carrier & diagonal)
+        spread_q(diagonal)
+
+    def service_2():
+        ct_copy(opposite, y, 2).wait_recv()
+        for d in range(1, 4):
+            send(lambda d=d: cx_copy(2, d))
+        cw_copy(down, y, 0).wait_recv()
+        send(lambda: cw_copy(down, up, 2), c == 0)
+        cw_copy(up, y, 1).wait_recv()
+        send(lambda: cw_copy(up, down, 2), c == 1)
+        for r in range(2):
+            send(lambda r=r: cw_other(r, half))
+
+    def service_3():
+        beside = (turn == 1) | (turn == 3)
+        when(carrier & beside, lambda: qb_copy(up, 0).wait_recv())
+        send(lambda: qb_copy(up, 2), carrier & (turn == 1) & (c == 0))
+        send(lambda: qb_copy(down, 2), carrier & (turn == 3) & (c == 1))
+        spread_q(beside)
+
+    services = {1: service_1, 2: service_2, 3: service_3}
 
     gi = lax.broadcasted_iota(jnp.int32, (C, 128), 0) - GROUP * lax.broadcasted_iota(jnp.int32, (C, 128), 1)
     gmat[...] = jnp.where((gi >= 0) & (gi < GROUP), 1.0, 0.0).astype(BF16)
@@ -214,33 +312,17 @@
         send(lambda k=k: lat_copy(z + k, 1), (z + k <= 3) & (z > 0))
         send(halo_up, (z + k == 3) & (y < 3))
         send(halo_down, (z - k == 0) & (y > 0))
+        services[k]()
         when(z - k >= 0, lambda k=k: activate(64 + BLK * (z - k), BLK))
         when(z + k <= 3, lambda k=k: activate(64 + BLK * (z + k), BLK))
 
-    cw_copy(down, y, 0).wait_recv()
-    send(lambda: cw_copy(down, up, 2), c == 0)
-    send(lambda: cw_forward(down, 0))
-    cw_copy(up, y, 1).wait_recv()
-    send(lambda: cw_copy(up, down, 2), c == 1)
-    send(lambda: cw_forward(up, 1))
-
-    for copy in loc[2:]:
-        copy.wait()
-
-    def qw_rows(k):
-        return pl.ds(pl.multiple_of(CB * k, 16), CB)
-
-    def qw_copy(yy, k, zz):
-        return remote(
-            wown.at[0:3, :, half], wqkv.at[:, qw_rows(k), half], s_qw.at[yy], r_qw.at[k], patch(yy, zz)
-        )
-
-    def qw_local():
-        return pltpu.make_async_copy(wown.at[0:3, :, half], wqkv.at[:, qw_rows(z), half], l_qw.at[0])
-
-    for yy in range(4):
-        send(lambda yy=yy: qw_copy(yy, z, y), (y != yy) | (z != y))
-    when(z == y, lambda: qw_local().start())
+    def wo_z(k, way):
+        zz = z + 1 if way == 0 else z - 1
+        ref = wo.at[4 * y + k, :, half]
+        return remote(ref, ref, s_woz.at[way, k], r_woz.at[k], patch(y, zz))
+
+    send(lambda: wo_z(z, 0), z < 3)
+    send(lambda: wo_z(z, 1), z > 0)
 
     when(y > 0, lambda: halo_up().wait_recv())
     when(y > 0, lambda: activate(0, 64))
@@ -257,10 +339,16 @@
     when(y == 3, zero_bottom)
 
     cw_copy(opposite, y, 2).wait_recv()
-    send(lambda: cw_forward(opposite, 2))
-    cw_arrival(down, 0).wait_recv()
-    cw_arrival(up, 1).wait_recv()
-    cw_arrival(opposite, 2).wait_recv()
+    send(lambda: cw_other(2, half))
+    for r in range(3):
+        for d in range(1, 4):
+            cx_from(r, d).wait_recv()
+        send(lambda r=r: ct_other(r, half))
+    when(carrier & (turn == 2), lambda: qb_copy(up, 0).wait_recv())
+    spread_q(turn == 2)
+    for r in range(3):
+        cw_other(r, other).wait_recv()
+        ct_other(r, other).wait_recv()
 
     bias = jnp.concatenate([st1[4 * yy + z, 15:16, 0:CB] for yy in range(4)], axis=1)
     CHUNK = 256
@@ -269,7 +357,7 @@
         total = jnp.zeros((CHUNK, 3 * CZ), F32)
         for dr in range(3):
             rows = pl.ds(pl.multiple_of(CHUNK * j + 64 * dr, 64), CHUNK)
-            total = total + dot_nt(act[rows], cw[dr].reshape(3 * CZ, C))
+            total = total + dot_nt(act[rows], cw[3 * dr : 3 * dr + 3].reshape(3 * CZ, C))
         ubuf[...] = total
         column = lax.broadcasted_iota(jnp.int32, (CHUNK, CZ), 0) % 64
         left = pltpu.roll(ubuf[:, 0:CZ], 1, 0)
@@ -306,19 +394,25 @@
         )
     st2[p] = st2s[...]
 
-    def qw_forward(k):
-        ref = wqkv.at[:, qw_rows(k), half]
-        return remote(ref, ref, s_qws.at[k], r_qws.at[k], sibling)
-
-    def qw_arrival(k):
-        ref = wqkv.at[:, qw_rows(k), other]
-        return remote(ref, ref, s_qws.at[k], r_qws.at[k], sibling)
-
-    for k in range(4):
-        remote_wait = (y != z) | (z != k)
-        when(remote_wait, lambda k=k: qw_copy(0, k, 0).wait_recv())
-        when(~remote_wait, lambda: qw_local().wait())
-        send(lambda k=k: qw_forward(k))
+    for k in range(1, 4):
+        when(z - k >= 0, lambda k=k: wo_z(z - k, 0).wait_recv())
+        send(lambda k=k: wo_z(z - k, 0), (z - k >= 0) & (z < 3))
+        when(z + k <= 3, lambda k=k: wo_z(z + k, 1).wait_recv())
+        send(lambda k=k: wo_z(z + k, 1), (z + k <= 3) & (z > 0))
+
+    def wo_row(src_y, mask):
+        return wo.at[pl.ds(4 * src_y, 4), :, mask]
+
+    def wo_y(src_y, to_y, slot):
+        ref = wo_row(src_y, half)
+        return remote(ref, ref, s_woy.at[slot], r_woy.at[slot], patch(to_y, z))
+
+    send(lambda: wo_y(y, up, 0))
+    send(lambda: wo_y(y, down, 1))
+    for d in range(1, 4):
+        when((x + 4 - d) % 4 < 3, lambda d=d: qc_from(d).wait_recv())
+    for m in range(3):
+        send(lambda m=m: qd_other(m, half))
 
     for d in range(1, 16):
         q = (p + 16 - d) % 16
@@ -346,14 +440,10 @@
         when(z + k <= 3, lambda k=k: hid_copy(z + k, 1).wait_recv())
         send(lambda k=k: hid_copy(z + k, 1), (z + k <= 3) & (z > 0))
 
-    def wo_z(k, way):
-        zz = z + 1 if way == 0 else z - 1
-        ref = wo.at[4 * y + k, :, half]
-        return remote(ref, ref, s_woz.at[way, k], r_woz.at[k], patch(y, zz))
-
-    send(lambda: wo_z(z, 0), z < 3)
-    send(lambda: wo_z(z, 1), z > 0)
-
+    wo_y(down, y, 0).wait_recv()
+    send(lambda: wo_y(down, up, 2), c == 0)
+    wo_y(up, y, 1).wait_recv()
+    send(lambda: wo_y(up, down, 2), c == 1)
     def normalize(i, carry):
         rows = pl.ds(pl.multiple_of(16 * i, 16), 16)
         blocks = [
@@ -367,8 +457,8 @@
 
     lax.fori_loop(0, ROWS_Y // 16, normalize, 0)
 
-    for k in range(4):
-        qw_arrival(k).wait_recv()
+    for m in range(3):
+        qd_other(m, other).wait_recv()
 
     def project(j, carry):
         rows = pl.ds(pl.multiple_of(256 * j, 256), 256)
@@ -398,26 +488,23 @@
 
     lax.fori_loop(0, BLK // 16, residual, 0)
 
-    for k in range(1, 4):
-        when(z - k >= 0, lambda k=k: wo_z(z - k, 0).wait_recv())
-        send(lambda k=k: wo_z(z - k, 0), (z - k >= 0) & (z < 3))
-        when(z + k <= 3, lambda k=k: wo_z(z + k, 1).wait_recv())
-        send(lambda k=k: wo_z(z + k, 1), (z + k <= 3) & (z > 0))
-
+    wo_y(opposite, y, 2).wait_recv()
+
+    def wo_forward(k):
+        ref = wo_row(k, half)
+        return remote(ref, ref, s_wos.at[k], r_wos.at[k], sibling)
+
+    def wo_arrival(k):
+        ref = wo_row(k, other)
+        return remote(ref, ref, s_wos.at[k], r_wos.at[k], sibling)
+
+    for k in range(4):
+        send(lambda k=k: wo_forward(k))
     kv_copy(0, down, y, 0).wait_recv()
     send(lambda: kv_copy(0, down, up, 2))
     kv_copy(1, up, y, 1).wait_recv()
     send(lambda: kv_copy(1, up, down, 2))
 
-    def wo_row(src_y, mask):
-        return wo.at[pl.ds(4 * src_y, 4), :, mask]
-
-    def wo_y(src_y, to_y, slot):
-        ref = wo_row(src_y, half)
-        return remote(ref, ref, s_woy.at[slot], r_woy.at[slot], patch(to_y, z))
-
-    send(lambda: wo_y(y, up, 0))
-    send(lambda: wo_y(y, down, 1))
     kv_copy(1, down, y, 0).wait_recv()
     kv_copy(0, up, y, 1).wait_recv()
     kv_copy(0, opposite, y, 2).wait_recv()
@@ -463,22 +550,6 @@
     for k in range(4):
         pending.append((z != k, lambda k=k: att_copy(k)))
 
-    wo_y(down, y, 0).wait_recv()
-    send(lambda: wo_y(down, up, 2), c == 0)
-    wo_y(up, y, 1).wait_recv()
-    send(lambda: wo_y(up, down, 2), c == 1)
-    wo_y(opposite, y, 2).wait_recv()
-
-    def wo_forward(k):
-        ref = wo_row(k, half)
-        return remote(ref, ref, s_wos.at[k], r_wos.at[k], sibling)
-
-    def wo_arrival(k):
-        ref = wo_row(k, other)
-        return remote(ref, ref, s_wos.at[k], r_wos.at[k], sibling)
-
-    for k in range(4):
-        send(lambda k=k: wo_forward(k))
     for k in range(4):
         wo_arrival(k).wait_recv()
     for k in range(4):
@@ -503,7 +574,7 @@
         scratch_shapes=[
             pltpu.VMEM((640, C), BF16),
             pltpu.VMEM((640, C), BF16),
-            pltpu.VMEM((3, 3, 4, CB, C), BF16),
+            pltpu.VMEM((9, 4, CB, C), BF16),
             pltpu.VMEM((4, CB, C), BF16),
             pltpu.VMEM((3, CZ, C), BF16),
             pltpu.VMEM((16, CB, C), BF16),
@@ -526,7 +597,8 @@
             pltpu.VMEM((4, BLK, CZ), BF16),
             dma((7,)), dma((16,)), dma((16,)), dma((2, 4)), dma((4,)), dma((2,)), dma((2,)),
             dma((3,)), dma((3,)), dma((3,)), dma((3,)),
-            dma((4,)), dma((4,)), dma((4,)), dma((4,)), dma((1,)),
+            dma((3,)), dma((3,)), dma((3, 4)), dma((3, 4)), dma((3,)), dma((3,)),
+            dma((1,)), dma((4,)), dma((1,)), dma((3,)), dma((1,)), dma((4,)), dma((4,)), dma((3,)), dma((3,)),
             dma((2, 4)), dma((4,)), dma((3,)), dma((3,)), dma((4,)), dma((4,)),
             dma((16,)), dma((16,)), dma((2, 4)), dma((4,)), dma((2, 3)), dma((2, 3)), dma((4,)), dma((4,)),
         ],
@@ -534,7 +606,7 @@
             collective_id=0, has_side_effects=True, vmem_limit_bytes=60 * 1024 * 1024
         ),
     )(
-        latent.reshape(BLK, C), conv_weight, channel_bias.reshape(1, CB), w_query, w_key, w_value, w_out
+        latent.reshape(BLK, C), conv_weight.reshape(9, CB, C), channel_bias.reshape(1, CB), w_query, w_key, w_value, w_out
     )
     return out.reshape(latent.shape)
 

time: 222 us -> 147 us (0.66)
  Pallas kernels: 218 us -> 144 us
    pallas_call x1, Pallas kernels: 218 us -> 144 us  [on_device(): pl.pallas_call(kernel, out_shape=jax.ShapeDtypeStruct((BLK, C), BF16), in...]
where the time goes in v2:
time: 147 us; the launch traced here: 146 us
  Pallas kernels  144 us (98%)
  local copies, waits for them, and re-layouts  1.72 us (1%)
    pallas_call x1, Pallas kernels, on_device(): pl.pallas_call(kernel, out_shape=jax.ShapeDtypeStruct((BLK, C), BF16), in...  144 us

profile of v2, /device:TPU:8, one launch (start us, length us, event | category | flops | bytes accessed | tf_op | source)
XLA Modules:
  0.0 145.9 jit_solution(13979511858625556701)
XLA Ops:
  0.0 144.2 %shard_map.73 = bf16[128,1280]{1,0:T(8,128)(2,1)} custom-call(bf16[128,1280]{1,0:T(8,128)(2,1)} %bitcast.6, bf16[9,80,1280]{2,1,0:T(8,128)(2,1)} %bitcast.4, f32[1,80]{1,0:T(1,128)} %bitcast.7, bf16[80,1280]{1,0:T(8,128)(2,1)} %wq_in.1, bf16[80,1280]{1,0:T(8,128)(2,1)} %wk_in.1, bf16[80,1280]{1,0:T(8,128)(2,1)} %wv_in.1, bf16[80,1280]{1,0:T(8,128)(2,1)} %wo_in.1), custom_call_target="tpu_custom_call" | custom-call | tf_op jit(solution)/shard_map/pallas_call | solution.py:569
  144.2 1.7 %copy.9 = bf16[2,64,1280]{2,1,0:T(8,128)(2,1)} copy(bf16[2,64,1280]{2,1,0:T(8,128)(2,1)} %bitcast.5) | data formatting | bytes 655360

commit v3 on v2

--- a/solution.py
+++ b/solution.py
@@ -13,6 +13,10 @@
 NY, NZ = 4, 4
 BLK = 128
 ROWS_Y = 512
+NCH = 4
+R = ROWS_Y // NCH
+HALF = R // 2
+AHEAD = 1
 CB = C // 16
 CZ = C // 4
 EPS = 1e-05
@@ -32,7 +36,7 @@
 def kernel(
     lat_in, cw_in, bias_in, wq_in, wk_in, wv_in, wo_in, out_ref,
     lat, act, cw, wown, wqkv, wo, st1s, st1, st2s, st2, gmat, gmat_t, sel,
-    gn1, gn2, ubuf, hidg, nrm, hnat, qb, kv, att, attg,
+    gn1, gn2, stc, ubuf, hidg, nrm, hnat, qb, kv, att, attg,
     s_loc, s_st1, r_st1, s_lat, r_lat, s_halo, r_halo, s_cw, r_cw, s_cws, r_cws,
     s_ct, r_ct, s_cx, r_cx, s_cts, r_cts,
     s_qa, r_qa, l_qa, s_qb, r_qb, s_qc, r_qc, s_qd, r_qd, s_woz, r_woz, s_woy, r_woy, s_wos, r_wos,
@@ -366,22 +370,38 @@
         value = value + jnp.where(column == 0, 0.0, left) + jnp.where(column == 63, 0.0, right)
         own = lat[pl.ds(pl.multiple_of(64 + CHUNK * j, 64), CHUNK)]
         value = value + dot_nn(own, sel[...]) + bias
-        hidg[z, pl.ds(pl.multiple_of(CHUNK * j, 128), CHUNK), :] = value.astype(BF16)
+        value = value.astype(BF16).astype(F32)
+        mean = jnp.sum(value, axis=0, keepdims=True) * (1.0 / CHUNK)
+        stc[j, 0:1, :] = mean
+        stc[j, 1:2, :] = jnp.sum(jnp.square(value - mean), axis=0, keepdims=True)
+        for i in range(CHUNK // R):
+            upper = value[R * i : R * i + HALF]
+            lower = value[R * i + HALF : R * i + R]
+            ch = (CHUNK // R) * j + i
+            hidg[z, ch, 0] = upper[:, 0:128].astype(BF16)
+            hidg[z, ch, 1] = upper[:, 128:256].astype(BF16)
+            hidg[z, ch, 2] = lower[:, 0:128].astype(BF16)
+            hidg[z, ch, 3] = lower[:, 128:256].astype(BF16)
+            hidg[z, ch, 4] = jnp.concatenate([upper[:, 256:CZ], lower[:, 256:CZ]], axis=1).astype(BF16)
         return carry
 
-    lax.fori_loop(0, ROWS_Y // CHUNK, conv_chunk, 0)
-
-    def hid_copy(k, way):
+    def hid_copy(ch, k, way):
         zz = z + 1 if way == 0 else z - 1
-        return remote(hidg.at[k], hidg.at[k], s_hid.at[way, k], r_hid.at[k], patch(y, zz))
-
-    send(lambda: hid_copy(z, 0), z < 3)
-    send(lambda: hid_copy(z, 1), z > 0)
+        ref = hidg.at[k, ch]
+        return remote(ref, ref, s_hid.at[way, ch, k], r_hid.at[ch, k], patch(y, zz))
+
+    def hid_own(ch):
+        send(lambda: hid_copy(ch, z, 0), z < 3)
+        send(lambda: hid_copy(ch, z, 1), z > 0)
+
+    conv_chunk(0, 0)
+    hid_own(0)
+    conv_chunk(1, 0)
 
     st2s[...] = jnp.zeros_like(st2s)
-    hidden = hidg[z].astype(F32)
-    mean = jnp.sum(hidden, axis=0, keepdims=True) * (1.0 / ROWS_Y)
-    m2 = jnp.sum(jnp.square(hidden - mean), axis=0, keepdims=True)
+    mean = 0.5 * (stc[0, 0:1, :] + stc[1, 0:1, :])
+    m2 = stc[0, 1:2, :] + stc[1, 1:2, :]
+    m2 = m2 + CHUNK * (jnp.square(stc[0, 0:1, :] - mean) + jnp.square(stc[1, 0:1, :] - mean))
     for j in range(3):
         width = min(128, CZ - 128 * j)
         st2s[j : j + 1, 0:width] = mean[:, 128 * j : 128 * j + width]
@@ -394,12 +414,6 @@
         )
     st2[p] = st2s[...]
 
-    for k in range(1, 4):
-        when(z - k >= 0, lambda k=k: wo_z(z - k, 0).wait_recv())
-        send(lambda k=k: wo_z(z - k, 0), (z - k >= 0) & (z < 3))
-        when(z + k <= 3, lambda k=k: wo_z(z + k, 1).wait_recv())
-        send(lambda k=k: wo_z(z + k, 1), (z + k <= 3) & (z > 0))
-
     def wo_row(src_y, mask):
         return wo.at[pl.ds(4 * src_y, 4), :, mask]
 
@@ -407,87 +421,130 @@
         ref = wo_row(src_y, half)
         return remote(ref, ref, s_woy.at[slot], r_woy.at[slot], patch(to_y, z))
 
-    send(lambda: wo_y(y, up, 0))
-    send(lambda: wo_y(y, down, 1))
-    for d in range(1, 4):
-        when((x + 4 - d) % 4 < 3, lambda d=d: qc_from(d).wait_recv())
-    for m in range(3):
-        send(lambda m=m: qd_other(m, half))
-
-    for d in range(1, 16):
-        q = (p + 16 - d) % 16
-        remote(st2s, st2.at[q], s_st2.at[d], r_st2.at[d], {"batch": b, "patch": q}).wait_recv()
-    parts = [[st2[4 * yy + zz] for zz in range(4)] for yy in range(4)]
-    mean_rows, m2_rows = [], []
-    for zz in range(4):
-        col = [parts[yy][zz] for yy in range(4)]
-        m = (col[0] + col[1] + col[2] + col[3]) * 0.25
-        dev = sum(jnp.square(x - m) for x in col)
-        total = col[0] + col[1] + col[2] + col[3]
-        m2_all = total[4:8] + ROWS_Y * dev[0:4]
-        mean_rows.append(to_lanes(m, 3)[:, 0:CZ])
-        m2_rows.append(to_lanes(m2_all, 3)[:, 0:CZ])
-    mean_l = jnp.concatenate(mean_rows + mean_rows, axis=0)
-    m2_l = jnp.concatenate(m2_rows + m2_rows, axis=0)
-    centre = group_sums(mean_l) * (1.0 / GROUP)
-    spread = group_sums(m2_l + 2048.0 * jnp.square(mean_l - centre)) * (1.0 / (2048 * GROUP))
-    gn2[0] = centre
-    gn2[1] = lax.rsqrt(spread + EPS)
-
-    for k in range(1, 4):
-        when(z - k >= 0, lambda k=k: hid_copy(z - k, 0).wait_recv())
-        send(lambda k=k: hid_copy(z - k, 0), (z - k >= 0) & (z < 3))
-        when(z + k <= 3, lambda k=k: hid_copy(z + k, 1).wait_recv())
-        send(lambda k=k: hid_copy(z + k, 1), (z + k <= 3) & (z > 0))
-
-    wo_y(down, y, 0).wait_recv()
-    send(lambda: wo_y(down, up, 2), c == 0)
-    wo_y(up, y, 1).wait_recv()
-    send(lambda: wo_y(up, down, 2), c == 1)
-    def normalize(i, carry):
-        rows = pl.ds(pl.multiple_of(16 * i, 16), 16)
-        blocks = [
-            (hidg[zz, rows, :].astype(F32) - gn2[0, zz : zz + 1, :]) * gn2[1, zz : zz + 1, :]
-            for zz in range(4)
-        ]
-        nrm[rows] = jnp.concatenate(
+    def weights_1():
+        for k in range(1, 4):
+            when(z - k >= 0, lambda k=k: wo_z(z - k, 0).wait_recv())
+            send(lambda k=k: wo_z(z - k, 0), (z - k >= 0) & (z < 3))
+            when(z + k <= 3, lambda k=k: wo_z(z + k, 1).wait_recv())
+            send(lambda k=k: wo_z(z + k, 1), (z + k <= 3) & (z > 0))
+        send(lambda: wo_y(y, up, 0))
+        send(lambda: wo_y(y, down, 1))
+        for d in range(1, 4):
+            when((x + 4 - d) % 4 < 3, lambda d=d: qc_from(d).wait_recv())
+        for m in range(3):
+            send(lambda m=m: qd_other(m, half))
+
+    def second_norm():
+        for d in range(1, 16):
+            q = (p + 16 - d) % 16
+            remote(st2s, st2.at[q], s_st2.at[d], r_st2.at[d], {"batch": b, "patch": q}).wait_recv()
+        parts = [[st2[4 * yy + zz] for zz in range(4)] for yy in range(4)]
+        mean_rows, m2_rows = [], []
+        for zz in range(4):
+            col = [parts[yy][zz] for yy in range(4)]
+            m = (col[0] + col[1] + col[2] + col[3]) * 0.25
+            dev = sum(jnp.square(x - m) for x in col)
+            total = col[0] + col[1] + col[2] + col[3]
+            m2_all = total[4:8] + ROWS_Y * dev[0:4]
+            mean_rows.append(to_lanes(m, 3)[:, 0:CZ])
+            m2_rows.append(to_lanes(m2_all, 3)[:, 0:CZ])
+        mean_l = jnp.concatenate(mean_rows + mean_rows, axis=0)
+        m2_l = jnp.concatenate(m2_rows + m2_rows, axis=0)
+        centre = group_sums(mean_l) * (1.0 / GROUP)
+        spread = group_sums(m2_l + 2048.0 * jnp.square(mean_l - centre)) * (1.0 / (2048 * GROUP))
+        gn2[0] = centre
+        gn2[1] = lax.rsqrt(spread + EPS)
+
+    def hidden_rows(zz, ch, h, rows):
+        tail = hidg[zz, ch, 4, rows, :].astype(F32)[:, 64 * h : 64 * h + 64]
+        return jnp.concatenate(
+            [hidg[zz, ch, 2 * h, rows, :].astype(F32), hidg[zz, ch, 2 * h + 1, rows, :].astype(F32), tail],
+            axis=1,
+        )
+
+    def in_order(blocks):
+        return jnp.concatenate(
             [blocks[zz][:, CB * yy : CB * yy + CB] for yy in range(4) for zz in range(4)], axis=1
+        )
+
+    def normalize(ch):
+        for h in range(2):
+            def body(i, carry, h=h):
+                rows = pl.ds(pl.multiple_of(16 * i, 16), 16)
+                blocks = [
+                    (hidden_rows(zz, ch, h, rows) - gn2[0, zz : zz + 1, :]) * gn2[1, zz : zz + 1, :]
+                    for zz in range(4)
+                ]
+                nrm[pl.ds(pl.multiple_of(HALF * h + 16 * i, 16), 16)] = in_order(blocks).astype(BF16)
+                return carry
+
+            lax.fori_loop(0, HALF // 16, body, 0)
+
+    def project(ch):
+        rows = pl.ds(R * ch, R)
+        both = dot_nt(nrm[...], wqkv[...].reshape(3 * CZ, C))
+        kv[y, rows, 0:256] = both[:, CZ : CZ + 256].astype(BF16)
+        kv[y, rows, 256:512] = both[:, 2 * CZ : 2 * CZ + 256].astype(BF16)
+        kv[y, rows, 512:640] = jnp.concatenate(
+            [both[:, CZ + 256 : 2 * CZ], both[:, 2 * CZ + 256 : 3 * CZ]], axis=1
         ).astype(BF16)
-        return carry
-
-    lax.fori_loop(0, ROWS_Y // 16, normalize, 0)
-
-    for m in range(3):
-        qd_other(m, other).wait_recv()
-
-    def project(j, carry):
-        rows = pl.ds(pl.multiple_of(256 * j, 256), 256)
-        block = nrm[rows]
-        kv[0, y, rows, :] = dot_nt(block, wqkv[1]).astype(BF16)
-        kv[1, y, rows, :] = dot_nt(block, wqkv[2]).astype(BF16)
-        qb[rows] = (dot_nt(block, wqkv[0]).astype(BF16).astype(F32) * HEAD_DIM**-0.5).astype(BF16)
-        return carry
-
-    lax.fori_loop(0, ROWS_Y // 256, project, 0)
-
-    def kv_copy(which, src_y, to_y, slot):
-        ref = kv.at[which, src_y]
-        return remote(ref, ref, s_kv.at[which, slot], r_kv.at[which, slot], patch(to_y, z))
-
-    for which in range(2):
-        send(lambda which=which: kv_copy(which, y, up, 0))
-        send(lambda which=which: kv_copy(which, y, down, 1))
-
-    def residual(i, carry):
-        rows = pl.ds(pl.multiple_of(BLK * z + 16 * i, 16), 16)
-        blocks = [hidg[zz, rows, :].astype(F32) for zz in range(4)]
-        hnat[pl.ds(pl.multiple_of(16 * i, 16), 16)] = jnp.concatenate(
-            [blocks[zz][:, CB * yy : CB * yy + CB] for yy in range(4) for zz in range(4)], axis=1
-        )
-        return carry
-
-    lax.fori_loop(0, BLK // 16, residual, 0)
-
+        query = (both[:, 0:CZ].astype(BF16).astype(F32) * HEAD_DIM**-0.5).astype(BF16)
+        qb[rows, 0:256] = query[:, 0:256]
+        qb[rows, 256:384] = jnp.concatenate(
+            [query[:, 256:CZ].astype(F32), jnp.zeros((R, 64), F32)], axis=1
+        ).astype(BF16)
+
+    def kv_copy(ch, h, src_y, to_y, slot):
+        ref = kv.at[src_y, pl.ds(R * ch + HALF * h, HALF), :]
+        return remote(ref, ref, s_kv.at[ch, h, slot], r_kv.at[ch, h, slot], patch(to_y, z))
+
+    def kv_own(ch):
+        send(lambda: kv_copy(ch, 0, y, up, 0))
+        send(lambda: kv_copy(ch, 1, y, down, 1))
+        send(lambda: kv_copy(ch, 1, y, up, 0))
+        send(lambda: kv_copy(ch, 0, y, down, 1))
+
+    def kv_on(ch):
+        kv_copy(ch, 0, down, y, 0).wait_recv()
+        send(lambda: kv_copy(ch, 0, down, up, 2))
+        kv_copy(ch, 1, up, y, 1).wait_recv()
+        send(lambda: kv_copy(ch, 1, up, down, 2))
+
+    for ch in range(NCH):
+        for k in range(1, 4):
+            when(z - k >= 0, lambda k=k, ch=ch: hid_copy(ch, z - k, 0).wait_recv())
+            send(lambda k=k, ch=ch: hid_copy(ch, z - k, 0), (z - k >= 0) & (z < 3))
+            when(z + k <= 3, lambda k=k, ch=ch: hid_copy(ch, z + k, 1).wait_recv())
+            send(lambda k=k, ch=ch: hid_copy(ch, z + k, 1), (z + k <= 3) & (z > 0))
+            if k == AHEAD and ch + 1 < NCH:
+                hid_own(ch + 1)
+            if ch == 0 and k == 2:
+                weights_1()
+        if ch == 0:
+            second_norm()
+            for m in range(3):
+                qd_other(m, other).wait_recv()
+        if ch == 1:
+            wo_y(down, y, 0).wait_recv()
+            send(lambda: wo_y(down, up, 2), c == 0)
+            wo_y(up, y, 1).wait_recv()
+            send(lambda: wo_y(up, down, 2), c == 1)
+        normalize(ch)
+        project(ch)
+        kv_own(ch)
+        if ch > 0:
+            kv_on(ch - 1)
+
+    for h in range(2):
+        def residual(i, carry, h=h):
+            rows = pl.ds(pl.multiple_of(16 * i, 16), 16)
+            blocks = [hidden_rows(zz, z, h, rows) for zz in range(4)]
+            hnat[pl.ds(pl.multiple_of(HALF * h + 16 * i, 16), 16)] = in_order(blocks)
+            return carry
+
+        lax.fori_loop(0, HALF // 16, residual, 0)
+
+    kv_on(NCH - 1)
     wo_y(opposite, y, 2).wait_recv()
 
     def wo_forward(k):
@@ -500,15 +557,11 @@
 
     for k in range(4):
         send(lambda k=k: wo_forward(k))
-    kv_copy(0, down, y, 0).wait_recv()
-    send(lambda: kv_copy(0, down, up, 2))
-    kv_copy(1, up, y, 1).wait_recv()
-    send(lambda: kv_copy(1, up, down, 2))
-
-    kv_copy(1, down, y, 0).wait_recv()
-    kv_copy(0, up, y, 1).wait_recv()
-    kv_copy(0, opposite, y, 2).wait_recv()
-    kv_copy(1, opposite, y, 2).wait_recv()
+    for ch in range(NCH):
+        kv_copy(ch, 1, down, y, 0).wait_recv()
+        kv_copy(ch, 0, up, y, 1).wait_recv()
+        kv_copy(ch, 0, opposite, y, 2).wait_recv()
+        kv_copy(ch, 1, opposite, y, 2).wait_recv()
 
     def att_copy(j):
         return remote(att.at[j], attg.at[z], s_att.at[j], r_att.at[z], patch(y, j))
@@ -521,10 +574,12 @@
         for pair in range(3):
             width = min(128, CZ - 128 * pair)
             lanes = slice(128 * pair, 128 * pair + width)
-            query = qb[rows, lanes]
-            keys = kv[0, :, :, lanes].reshape(2048, width)
-            values = kv[1, :, :, lanes].reshape(2048, width)
-            lane = lax.broadcasted_iota(jnp.int32, (BLK, width), 1)
+            query = qb[rows, 128 * pair : 128 * pair + 128]
+            key_at = 128 * pair if pair < 2 else 512
+            value_at = key_at + 256 if pair < 2 else 512
+            keys = kv[:, :, key_at : key_at + 128].reshape(2048, 128)
+            values = kv[:, :, value_at : value_at + 128].reshape(2048, 128)
+            lane = lax.broadcasted_iota(jnp.int32, (BLK, 128), 1)
             result = None
             for side in range(width // 64):
                 q1 = query
@@ -537,6 +592,8 @@
                 row_total = jnp.sum(unnormalized, axis=1, keepdims=True)
                 mix = dot_nn(unnormalized.astype(BF16), values) / row_total
                 result = mix if result is None else jnp.where(lane < 64, result, mix)
+            if width == 64:
+                result = result[:, 64:128]
             att[j, :, lanes] = result.astype(BF16)
 
     def attend_step(t, carry):
@@ -587,12 +644,13 @@
             pltpu.VMEM((C, CZ), BF16),
             pltpu.VMEM((2, 8, C), F32),
             pltpu.VMEM((2, 8, CZ), F32),
+            pltpu.VMEM((2, 8, CZ), F32),
             pltpu.VMEM((256, 3 * CZ), F32),
-            pltpu.VMEM((4, ROWS_Y, CZ), BF16),
-            pltpu.VMEM((ROWS_Y, C), BF16),
+            pltpu.VMEM((4, NCH, 5, HALF, 128), BF16),
+            pltpu.VMEM((R, C), BF16),
             pltpu.VMEM((BLK, C), F32),
-            pltpu.VMEM((ROWS_Y, CZ), BF16),
-            pltpu.VMEM((2, 4, ROWS_Y, CZ), BF16),
+            pltpu.VMEM((ROWS_Y, 384), BF16),
+            pltpu.VMEM((4, ROWS_Y, 2 * CZ), BF16),
             pltpu.VMEM((4, BLK, CZ), BF16),
             pltpu.VMEM((4, BLK, CZ), BF16),
             dma((7,)), dma((16,)), dma((16,)), dma((2, 4)), dma((4,)), dma((2,)), dma((2,)),
@@ -600,7 +658,8 @@
             dma((3,)), dma((3,)), dma((3, 4)), dma((3, 4)), dma((3,)), dma((3,)),
             dma((1,)), dma((4,)), dma((1,)), dma((3,)), dma((1,)), dma((4,)), dma((4,)), dma((3,)), dma((3,)),
             dma((2, 4)), dma((4,)), dma((3,)), dma((3,)), dma((4,)), dma((4,)),
-            dma((16,)), dma((16,)), dma((2, 4)), dma((4,)), dma((2, 3)), dma((2, 3)), dma((4,)), dma((4,)),
+            dma((16,)), dma((16,)), dma((2, NCH, 4)), dma((NCH, 4)), dma((NCH, 2, 3)), dma((NCH, 2, 3)),
+            dma((4,)), dma((4,)),
         ],
         compiler_params=pltpu.CompilerParams(
             collective_id=0, has_side_effects=True, vmem_limit_bytes=60 * 1024 * 1024

time: 147 us -> 130 us (0.88)
  Pallas kernels: 144 us -> 127 us
    pallas_call x1, Pallas kernels: 144 us -> 127 us  [on_device(): pl.pallas_call(kernel, out_shape=jax.ShapeDtypeStruct((BLK, C), BF16), in...]
where the time goes in v3:
time: 130 us; the launch traced here: 129 us
  Pallas kernels  127 us (98%)
  local copies, waits for them, and re-layouts  1.72 us (1%)
    pallas_call x1, Pallas kernels, on_device(): pl.pallas_call(kernel, out_shape=jax.ShapeDtypeStruct((BLK, C), BF16), in...  127 us

profile of v3, /device:TPU:8, one launch (start us, length us, event | category | flops | bytes accessed | tf_op | source)
XLA Modules:
  0.0 129.1 jit_solution(7860574121868402121)
XLA Ops:
  0.0 127.4 %shard_map.73 = bf16[128,1280]{1,0:T(8,128)(2,1)} custom-call(bf16[128,1280]{1,0:T(8,128)(2,1)} %bitcast.6, bf16[9,80,1280]{2,1,0:T(8,128)(2,1)} %bitcast.4, f32[1,80]{1,0:T(1,128)} %bitcast.7, bf16[80,1280]{1,0:T(8,128)(2,1)} %wq_in.1, bf16[80,1280]{1,0:T(8,128)(2,1)} %wk_in.1, bf16[80,1280]{1,0:T(8,128)(2,1)} %wv_in.1, bf16[80,1280]{1,0:T(8,128)(2,1)} %wo_in.1), custom_call_target="tpu_custom_call" | custom-call | tf_op jit(solution)/shard_map/pallas_call | solution.py:626
  127.4 1.7 %copy.9 = bf16[2,64,1280]{2,1,0:T(8,128)(2,1)} copy(bf16[2,64,1280]{2,1,0:T(8,128)(2,1)} %bitcast.5) | data formatting | bytes 655360

commit v4 on v3

--- a/solution.py
+++ b/solution.py
@@ -39,7 +39,7 @@
     gn1, gn2, stc, ubuf, hidg, nrm, hnat, qb, kv, att, attg,
     s_loc, s_st1, r_st1, s_lat, r_lat, s_halo, r_halo, s_cw, r_cw, s_cws, r_cws,
     s_ct, r_ct, s_cx, r_cx, s_cts, r_cts,
-    s_qa, r_qa, l_qa, s_qb, r_qb, s_qc, r_qc, s_qd, r_qd, s_woz, r_woz, s_woy, r_woy, s_wos, r_wos,
+    s_qa, r_qa, l_qa, s_qb, r_qb, s_qc, r_qc, s_qd, r_qd, s_woz, r_woz, s_woy, r_woy, s_wox, r_wox, s_wos, r_wos,
     s_st2, r_st2, s_hid, r_hid, s_kv, r_kv, s_att, r_att,
 ):
     p = lax.axis_index("patch")
@@ -87,7 +87,6 @@
         pltpu.make_async_copy(wk_in, wown.at[1], s_loc.at[3]),
         pltpu.make_async_copy(wv_in, wown.at[2], s_loc.at[4]),
         pltpu.make_async_copy(wo_in, wown.at[3], s_loc.at[5]),
-        pltpu.make_async_copy(wo_in.at[:, half], wo.at[p, :, half], s_loc.at[6]),
     ]
     for copy in loc:
         copy.start()
@@ -148,13 +147,27 @@
         ref = cw.at[5 + x, src_y, :, half]
         return remote(ref, ref, s_ct.at[slot], r_ct.at[slot], patch(to_y, z))
 
-    def cx_copy(r, d):
-        ref = cw.at[5 + x, around[r], :, half]
-        return remote(ref, ref, s_cx.at[r, d], r_cx.at[r, d], across(d))
-
-    def cx_from(r, d):
-        ref = cw.at[5 + (x + 4 - d) % 4, around[r], :, half]
-        return remote(ref, ref, s_cx.at[r, d], r_cx.at[r, d], across(d))
+    nexts = ((x + 1) % 4, (x + 3) % 4, (x + 2) % 4)
+
+    def x_send(ref, ssem, rsem):
+        send(lambda: remote(ref(x), ref(x), ssem(0), rsem(1), across(1)))
+        send(lambda: remote(ref(x), ref(x), ssem(1), rsem(0), across(3)))
+
+    def x_wait(ref, ssem, rsem, i):
+        remote(ref(nexts[i]), ref(nexts[i]), ssem(i), rsem(i), across(1)).wait_recv()
+
+    def x_relay(ref, ssem, rsem):
+        x_wait(ref, ssem, rsem, 1)
+        send(lambda: remote(ref(nexts[1]), ref(nexts[1]), ssem(2), rsem(2), across(1)), c == 0)
+        x_wait(ref, ssem, rsem, 0)
+        send(lambda: remote(ref(nexts[0]), ref(nexts[0]), ssem(2), rsem(2), across(3)), c == 1)
+
+    def cx(r):
+        return (
+            lambda i: cw.at[5 + i, around[r], :, half],
+            lambda i: s_cx.at[r, i],
+            lambda i: r_cx.at[r, i],
+        )
 
     def ct_other(r, mask):
         ref = cw.at[5:9, around[r], :, mask]
@@ -165,40 +178,29 @@
 
     for copy in loc[2:]:
         copy.wait()
-    carrier = x < 3
+    carrier = z == x
     diagonal = y == z
     turn = (y - z + 4) % 4
 
-    def qa_rows(k):
-        return wqkv.at[x, pl.ds(pl.multiple_of(CB * k, 16), CB), half]
-
-    def qa_copy(k):
-        return remote(wown.at[x, :, half], qa_rows(k), s_qa.at[0], r_qa.at[k], patch(y, y))
+    def q_ref(i):
+        return wqkv.at[:, pl.ds(pl.multiple_of(CB * i, 16), CB), half]
+
+    def qa_copy():
+        return remote(wown.at[0:3, :, half], q_ref(x), s_qa.at[0], r_qa.at[0], patch(y, y))
 
     def qa_local():
-        return pltpu.make_async_copy(wown.at[x, :, half], qa_rows(z), l_qa.at[0])
+        return pltpu.make_async_copy(wown.at[0:3, :, half], q_ref(x), l_qa.at[0])
 
     def qb_copy(to_y, slot):
-        ref = wqkv.at[x, :, half]
-        return remote(ref, ref, s_qb.at[slot], r_qb.at[0], patch(to_y, z))
-
-    def qc_copy(d):
-        ref = wqkv.at[x, :, half]
-        return remote(ref, ref, s_qc.at[d], r_qc.at[d], across(d))
-
-    def qc_from(d):
-        ref = wqkv.at[(x + 4 - d) % 4, :, half]
-        return remote(ref, ref, s_qc.at[d], r_qc.at[d], across(d))
-
-    def qd_other(m, mask):
-        ref = wqkv.at[m, :, mask]
-        return remote(ref, ref, s_qd.at[m], r_qd.at[m], sibling)
-
-    def spread_q(cond):
-        for d in range(1, 4):
-            send(lambda d=d: qc_copy(d), carrier & cond)
-
-    send(lambda: qa_copy(z), carrier & (z != y))
+        return remote(q_ref(x), q_ref(x), s_qb.at[slot], r_qb.at[0], patch(to_y, z))
+
+    qc = (q_ref, lambda i: s_qc.at[i], lambda i: r_qc.at[i])
+
+    def qd_other(mask):
+        ref = wqkv.at[:, :, mask]
+        return remote(ref, ref, s_qd.at[0], r_qd.at[0], sibling)
+
+    send(qa_copy, carrier & (z != y))
     when(carrier & diagonal, lambda: qa_local().start())
     send(lambda: cw_copy(y, up, 0))
     send(lambda: cw_copy(y, down, 1))
@@ -209,32 +211,32 @@
         ct_copy(up, y, 1).wait_recv()
         send(lambda: ct_copy(up, down, 2), c == 1)
         for r in range(2):
-            for d in range(1, 4):
-                send(lambda r=r, d=d: cx_copy(r, d))
-        for k in range(4):
-            when(carrier & diagonal & (z != k), lambda k=k: qa_copy(k).wait_recv())
-        when(carrier & diagonal, lambda: qa_local().wait())
-        send(lambda: qb_copy(up, 0), carrier & diagonal)
-        send(lambda: qb_copy(down, 1), carrier & diagonal)
-        spread_q(diagonal)
+            x_send(*cx(r))
+        when(diagonal & (z != x), lambda: qa_copy().wait_recv())
+        when(diagonal & carrier, lambda: qa_local().wait())
+        send(lambda: qb_copy(up, 0), diagonal)
+        send(lambda: qb_copy(down, 1), diagonal)
 
     def service_2():
         ct_copy(opposite, y, 2).wait_recv()
-        for d in range(1, 4):
-            send(lambda d=d: cx_copy(2, d))
+        x_send(*cx(2))
         cw_copy(down, y, 0).wait_recv()
         send(lambda: cw_copy(down, up, 2), c == 0)
         cw_copy(up, y, 1).wait_recv()
         send(lambda: cw_copy(up, down, 2), c == 1)
         for r in range(2):
             send(lambda r=r: cw_other(r, half))
+        beside = (turn == 1) | (turn == 3)
+        when(beside, lambda: qb_copy(up, 0).wait_recv())
+        send(lambda: qb_copy(up, 2), (turn == 1) & (c == 0))
+        send(lambda: qb_copy(down, 2), (turn == 3) & (c == 1))
+        for r in range(2):
+            x_relay(*cx(r))
 
     def service_3():
-        beside = (turn == 1) | (turn == 3)
-        when(carrier & beside, lambda: qb_copy(up, 0).wait_recv())
-        send(lambda: qb_copy(up, 2), carrier & (turn == 1) & (c == 0))
-        send(lambda: qb_copy(down, 2), carrier & (turn == 3) & (c == 1))
-        spread_q(beside)
+        when(turn == 2, lambda: qb_copy(up, 0).wait_recv())
+        x_send(*qc)
+        x_relay(*cx(2))
 
     services = {1: service_1, 2: service_2, 3: service_3}
 
@@ -320,13 +322,19 @@
         when(z - k >= 0, lambda k=k: activate(64 + BLK * (z - k), BLK))
         when(z + k <= 3, lambda k=k: activate(64 + BLK * (z + k), BLK))
 
-    def wo_z(k, way):
-        zz = z + 1 if way == 0 else z - 1
-        ref = wo.at[4 * y + k, :, half]
-        return remote(ref, ref, s_woz.at[way, k], r_woz.at[k], patch(y, zz))
-
-    send(lambda: wo_z(z, 0), z < 3)
-    send(lambda: wo_z(z, 1), z > 0)
+    def wo_ref(yy, i):
+        return wo.at[yy, i, :, half]
+
+    def wo_local():
+        return pltpu.make_async_copy(wown.at[3, :, half], wo_ref(y, x), l_qa.at[1])
+
+    def wo_z(to_z, slot):
+        return remote(wo_ref(y, x), wo_ref(y, x), s_woz.at[slot], r_woz.at[0], patch(y, to_z))
+
+    when(carrier, lambda: wo_local().start())
+    when(carrier, lambda: wo_local().wait())
+    send(lambda: wo_z(z + 1, 0), carrier & (z < 3))
+    send(lambda: wo_z(z - 1, 1), carrier & (z > 0))
 
     when(y > 0, lambda: halo_up().wait_recv())
     when(y > 0, lambda: activate(0, 64))
@@ -345,11 +353,20 @@
     cw_copy(opposite, y, 2).wait_recv()
     send(lambda: cw_other(2, half))
     for r in range(3):
-        for d in range(1, 4):
-            cx_from(r, d).wait_recv()
+        x_wait(*cx(r), 2)
         send(lambda r=r: ct_other(r, half))
-    when(carrier & (turn == 2), lambda: qb_copy(up, 0).wait_recv())
-    spread_q(turn == 2)
+    x_relay(*qc)
+    when(z != x, lambda: wo_z(z, 0).wait_recv())
+    send(lambda: wo_z(z + 1, 0), (z > x) & (z < 3))
+    send(lambda: wo_z(z - 1, 1), (z < x) & (z > 0))
+
+    def wo_y(src_y, to_y, slot):
+        return remote(wo_ref(src_y, x), wo_ref(src_y, x), s_woy.at[slot], r_woy.at[slot], patch(to_y, z))
+
+    wox = (lambda i: wo.at[:, i, :, half], lambda i: s_wox.at[i], lambda i: r_wox.at[i])
+
+    send(lambda: wo_y(y, up, 0))
+    send(lambda: wo_y(y, down, 1))
     for r in range(3):
         cw_other(r, other).wait_recv()
         ct_other(r, other).wait_recv()
@@ -414,25 +431,13 @@
         )
     st2[p] = st2s[...]
 
-    def wo_row(src_y, mask):
-        return wo.at[pl.ds(4 * src_y, 4), :, mask]
-
-    def wo_y(src_y, to_y, slot):
-        ref = wo_row(src_y, half)
-        return remote(ref, ref, s_woy.at[slot], r_woy.at[slot], patch(to_y, z))
-
     def weights_1():
-        for k in range(1, 4):
-            when(z - k >= 0, lambda k=k: wo_z(z - k, 0).wait_recv())
-            send(lambda k=k: wo_z(z - k, 0), (z - k >= 0) & (z < 3))
-            when(z + k <= 3, lambda k=k: wo_z(z + k, 1).wait_recv())
-            send(lambda k=k: wo_z(z + k, 1), (z + k <= 3) & (z > 0))
-        send(lambda: wo_y(y, up, 0))
-        send(lambda: wo_y(y, down, 1))
-        for d in range(1, 4):
-            when((x + 4 - d) % 4 < 3, lambda d=d: qc_from(d).wait_recv())
-        for m in range(3):
-            send(lambda m=m: qd_other(m, half))
+        x_wait(*qc, 2)
+        send(lambda: qd_other(half))
+        wo_y(down, y, 0).wait_recv()
+        send(lambda: wo_y(down, up, 2), c == 0)
+        wo_y(up, y, 1).wait_recv()
+        send(lambda: wo_y(up, down, 2), c == 1)
 
     def second_norm():
         for d in range(1, 16):
@@ -522,13 +527,12 @@
                 weights_1()
         if ch == 0:
             second_norm()
-            for m in range(3):
-                qd_other(m, other).wait_recv()
+            qd_other(other).wait_recv()
         if ch == 1:
-            wo_y(down, y, 0).wait_recv()
-            send(lambda: wo_y(down, up, 2), c == 0)
-            wo_y(up, y, 1).wait_recv()
-            send(lambda: wo_y(up, down, 2), c == 1)
+            wo_y(opposite, y, 2).wait_recv()
+            x_send(*wox)
+        if ch == 3:
+            x_relay(*wox)
         normalize(ch)
         project(ch)
         kv_own(ch)
@@ -545,18 +549,12 @@
         lax.fori_loop(0, HALF // 16, residual, 0)
 
     kv_on(NCH - 1)
-    wo_y(opposite, y, 2).wait_recv()
-
-    def wo_forward(k):
-        ref = wo_row(k, half)
-        return remote(ref, ref, s_wos.at[k], r_wos.at[k], sibling)
-
-    def wo_arrival(k):
-        ref = wo_row(k, other)
-        return remote(ref, ref, s_wos.at[k], r_wos.at[k], sibling)
-
-    for k in range(4):
-        send(lambda k=k: wo_forward(k))
+    def wo_other(mask):
+        ref = wo.at[:, :, :, mask]
+        return remote(ref, ref, s_wos.at[0], r_wos.at[0], sibling)
+
+    x_wait(*wox, 2)
+    send(lambda: wo_other(half))
     for ch in range(NCH):
         kv_copy(ch, 1, down, y, 0).wait_recv()
         kv_copy(ch, 0, up, y, 1).wait_recv()
@@ -607,8 +605,7 @@
     for k in range(4):
         pending.append((z != k, lambda k=k: att_copy(k)))
 
-    for k in range(4):
-        wo_arrival(k).wait_recv()
+    wo_other(other).wait_recv()
     for k in range(4):
         when(z != k, lambda k=k: att_from(k).wait_recv())
 
@@ -634,7 +631,7 @@
             pltpu.VMEM((9, 4, CB, C), BF16),
             pltpu.VMEM((4, CB, C), BF16),
             pltpu.VMEM((3, CZ, C), BF16),
-            pltpu.VMEM((16, CB, C), BF16),
+            pltpu.VMEM((4, 4, CB, C), BF16),
             pltpu.VMEM((32, 128), F32),
             pltpu.VMEM((16, 32, 128), F32),
             pltpu.VMEM((8, 128), F32),
@@ -653,11 +650,11 @@
             pltpu.VMEM((4, ROWS_Y, 2 * CZ), BF16),
             pltpu.VMEM((4, BLK, CZ), BF16),
             pltpu.VMEM((4, BLK, CZ), BF16),
-            dma((7,)), dma((16,)), dma((16,)), dma((2, 4)), dma((4,)), dma((2,)), dma((2,)),
+            dma((6,)), dma((16,)), dma((16,)), dma((2, 4)), dma((4,)), dma((2,)), dma((2,)),
             dma((3,)), dma((3,)), dma((3,)), dma((3,)),
             dma((3,)), dma((3,)), dma((3, 4)), dma((3, 4)), dma((3,)), dma((3,)),
-            dma((1,)), dma((4,)), dma((1,)), dma((3,)), dma((1,)), dma((4,)), dma((4,)), dma((3,)), dma((3,)),
-            dma((2, 4)), dma((4,)), dma((3,)), dma((3,)), dma((4,)), dma((4,)),
+            dma((1,)), dma((1,)), dma((2,)), dma((3,)), dma((1,)), dma((3,)), dma((3,)), dma((1,)), dma((1,)),
+            dma((2,)), dma((1,)), dma((3,)), dma((3,)), dma((3,)), dma((3,)), dma((1,)), dma((1,)),
             dma((16,)), dma((16,)), dma((2, NCH, 4)), dma((NCH, 4)), dma((NCH, 2, 3)), dma((NCH, 2, 3)),
             dma((4,)), dma((4,)),
         ],

time: 130 us -> 126 us (0.969); the launches traced: 129 us -> 123 us
  Pallas kernels: 127 us -> 122 us
    pallas_call x1, Pallas kernels: 127 us -> 122 us  [on_device(): pl.pallas_call(kernel, out_shape=jax.ShapeDtypeStruct((BLK, C), BF16), in...]
where the time goes in v4:
time: 126 us; the launch traced here: 123 us
  Pallas kernels  122 us (97%)
  local copies, waits for them, and re-layouts  1.72 us (1%)
    pallas_call x1, Pallas kernels, on_device(): pl.pallas_call(kernel, out_shape=jax.ShapeDtypeStruct((BLK, C), BF16), in...  122 us

profile of v4, /device:TPU:8, one launch (start us, length us, event | category | flops | bytes accessed | tf_op | source)
XLA Modules:
  0.0 123.4 jit_solution(10270864569737120676)
XLA Ops:
  0.0 121.7 %shard_map.73 = bf16[128,1280]{1,0:T(8,128)(2,1)} custom-call(bf16[128,1280]{1,0:T(8,128)(2,1)} %bitcast.6, bf16[9,80,1280]{2,1,0:T(8,128)(2,1)} %bitcast.4, f32[1,80]{1,0:T(1,128)} %bitcast.7, bf16[80,1280]{1,0:T(8,128)(2,1)} %wq_in.1, bf16[80,1280]{1,0:T(8,128)(2,1)} %wk_in.1, bf16[80,1280]{1,0:T(8,128)(2,1)} %wv_in.1, bf16[80,1280]{1,0:T(8,128)(2,1)} %wo_in.1), custom_call_target="tpu_custom_call" | custom-call | tf_op jit(solution)/shard_map/pallas_call | solution.py:623
  121.7 1.7 %copy.9 = bf16[2,64,1280]{2,1,0:T(8,128)(2,1)} copy(bf16[2,64,1280]{2,1,0:T(8,128)(2,1)} %bitcast.5) | data formatting | bytes 655360

commit v5 on v4

--- a/solution.py
+++ b/solution.py
@@ -99,15 +99,38 @@
     for d in range(1, 4):
         pl.semaphore_signal(barrier, inc=1, device_id=across(d), device_id_type=MESH)
 
+    gi = lax.broadcasted_iota(jnp.int32, (C, 128), 0) - GROUP * lax.broadcasted_iota(jnp.int32, (C, 128), 1)
+    gmat[...] = jnp.where((gi >= 0) & (gi < GROUP), 1.0, 0.0).astype(BF16)
+    ti = lax.broadcasted_iota(jnp.int32, (128, C), 1) - GROUP * lax.broadcasted_iota(jnp.int32, (128, C), 0)
+    gmat_t[...] = jnp.where((ti >= 0) & (ti < GROUP), 1.0, 0.0).astype(BF16)
+    def split_rows(x):
+        hi = x.astype(BF16).astype(F32)
+        mid = (x - hi).astype(BF16).astype(F32)
+        return jnp.concatenate([hi, mid, x - hi - mid], axis=0).astype(BF16)
+
+    def join_rows(x):
+        return x[0:8] + x[8:16] + x[16:24]
+
+    def to_groups(x):
+        return join_rows(dot_nn(split_rows(x), gmat[0 : x.shape[1], :]))
+
+    def to_channels(x, n):
+        return join_rows(dot_nn(split_rows(x), gmat_t[:, 0:n]))
+
+    def group_sums(x):
+        return to_channels(to_groups(x), x.shape[1])
+
     st1s[...] = jnp.zeros_like(st1s)
     loc[0].wait()
     mine = lat[own_rows].astype(F32)
     mean = jnp.sum(mine, axis=0, keepdims=True) * (1.0 / BLK)
     m2 = jnp.sum(jnp.square(mine - mean), axis=0, keepdims=True)
-    for j in range(10):
-        st1s[j : j + 1, :] = mean[:, 128 * j : 128 * j + 128]
-        st1s[16 + j : 17 + j, :] = m2[:, 128 * j : 128 * j + 128]
-    st1s[15:16, 0:CB] = bias_in[...]
+    mean = jnp.broadcast_to(mean, (8, C))
+    group_mean = to_groups(mean) * (1.0 / GROUP)
+    group_m2 = to_groups(m2 + BLK * jnp.square(mean - to_channels(group_mean, C)))
+    st1s[0:1, :] = group_mean[0:1, :]
+    st1s[1:2, :] = group_m2[0:1, :]
+    st1s[2:3, 0:CB] = bias_in[...]
 
     pl.semaphore_wait(barrier, 19)
 
@@ -212,10 +235,6 @@
         send(lambda: ct_copy(up, down, 2), c == 1)
         for r in range(2):
             x_send(*cx(r))
-        when(diagonal & (z != x), lambda: qa_copy().wait_recv())
-        when(diagonal & carrier, lambda: qa_local().wait())
-        send(lambda: qb_copy(up, 0), diagonal)
-        send(lambda: qb_copy(down, 1), diagonal)
 
     def service_2():
         ct_copy(opposite, y, 2).wait_recv()
@@ -226,60 +245,42 @@
         send(lambda: cw_copy(up, down, 2), c == 1)
         for r in range(2):
             send(lambda r=r: cw_other(r, half))
+        when(diagonal & (z != x), lambda: qa_copy().wait_recv())
+        when(diagonal & carrier, lambda: qa_local().wait())
+        send(lambda: qb_copy(up, 0), diagonal)
+        send(lambda: qb_copy(down, 1), diagonal)
+        for r in range(2):
+            x_relay(*cx(r))
+
+    def service_3():
         beside = (turn == 1) | (turn == 3)
         when(beside, lambda: qb_copy(up, 0).wait_recv())
         send(lambda: qb_copy(up, 2), (turn == 1) & (c == 0))
         send(lambda: qb_copy(down, 2), (turn == 3) & (c == 1))
-        for r in range(2):
-            x_relay(*cx(r))
-
-    def service_3():
-        when(turn == 2, lambda: qb_copy(up, 0).wait_recv())
-        x_send(*qc)
         x_relay(*cx(2))
 
     services = {1: service_1, 2: service_2, 3: service_3}
 
-    gi = lax.broadcasted_iota(jnp.int32, (C, 128), 0) - GROUP * lax.broadcasted_iota(jnp.int32, (C, 128), 1)
-    gmat[...] = jnp.where((gi >= 0) & (gi < GROUP), 1.0, 0.0).astype(BF16)
-    ti = lax.broadcasted_iota(jnp.int32, (128, C), 1) - GROUP * lax.broadcasted_iota(jnp.int32, (128, C), 0)
-    gmat_t[...] = jnp.where((ti >= 0) & (ti < GROUP), 1.0, 0.0).astype(BF16)
     for yy in range(4):
         rows = lax.broadcasted_iota(jnp.int32, (CZ, CZ), 0) - CB * z
         cols = lax.broadcasted_iota(jnp.int32, (CZ, CZ), 1) - CB * yy
         hit = (rows == cols) & (cols >= 0) & (cols < CB)
         sel[CZ * yy : CZ * yy + CZ, :] = jnp.where(hit, 1.0, 0.0).astype(BF16)
 
-    def split_rows(x):
-        hi = x.astype(BF16).astype(F32)
-        mid = (x - hi).astype(BF16).astype(F32)
-        return jnp.concatenate([hi, mid, x - hi - mid], axis=0).astype(BF16)
-
-    def join_rows(x):
-        return x[0:8] + x[8:16] + x[16:24]
-
-    def group_sums(x):
-        n = x.shape[1]
-        sums = join_rows(dot_nn(split_rows(x), gmat[0:n, :]))
-        return join_rows(dot_nn(split_rows(sums), gmat_t[:, 0:n]))
-
     for d in range(1, 16):
         q = (p + 16 - d) % 16
         remote(st1s, st1.at[q], s_st1.at[d], r_st1.at[d], {"batch": b, "patch": q}).wait_recv()
-    means = st1[:, 0:16, :]
-    mean_c = jnp.sum(means, axis=0) * (1.0 / 16)
-    m2_c = jnp.sum(st1[:, 16:32, :], axis=0) + BLK * jnp.sum(jnp.square(means - mean_c[None]), axis=0)
-
     def to_lanes(x, n):
         full = jnp.concatenate([x[j : j + 1, :] for j in range(n)], axis=1)
         return full
 
-    mean_l = jnp.broadcast_to(to_lanes(mean_c, 10), (8, C))
-    m2_l = jnp.broadcast_to(to_lanes(m2_c, 10), (8, C))
-    centre = group_sums(mean_l) * (1.0 / GROUP)
-    spread = group_sums(m2_l + 2048.0 * jnp.square(mean_l - centre)) * (1.0 / (2048 * GROUP))
-    gn1[0] = centre
-    gn1[1] = lax.rsqrt(spread + EPS)
+    stats = st1[...]
+    stats_sum = jnp.sum(stats, axis=0)
+    stats_dev = jnp.sum(jnp.square(stats - (stats_sum * (1.0 / 16))[None]), axis=0)
+    centre = stats_sum[0:1, :] * (1.0 / 16)
+    spread = (stats_sum[1:2, :] + (BLK * GROUP) * stats_dev[0:1, :]) * (1.0 / (2048 * GROUP))
+    gn1[0] = to_channels(jnp.broadcast_to(centre, (8, 128)), C)
+    gn1[1] = to_channels(jnp.broadcast_to(lax.rsqrt(spread + EPS), (8, 128)), C)
 
     def activate(start, count):
         def body(i, carry):
@@ -355,23 +356,19 @@
     for r in range(3):
         x_wait(*cx(r), 2)
         send(lambda r=r: ct_other(r, half))
-    x_relay(*qc)
-    when(z != x, lambda: wo_z(z, 0).wait_recv())
-    send(lambda: wo_z(z + 1, 0), (z > x) & (z < 3))
-    send(lambda: wo_z(z - 1, 1), (z < x) & (z > 0))
 
     def wo_y(src_y, to_y, slot):
         return remote(wo_ref(src_y, x), wo_ref(src_y, x), s_woy.at[slot], r_woy.at[slot], patch(to_y, z))
 
     wox = (lambda i: wo.at[:, i, :, half], lambda i: s_wox.at[i], lambda i: r_wox.at[i])
 
-    send(lambda: wo_y(y, up, 0))
-    send(lambda: wo_y(y, down, 1))
+    when(turn == 2, lambda: qb_copy(up, 0).wait_recv())
+    x_send(*qc)
     for r in range(3):
         cw_other(r, other).wait_recv()
         ct_other(r, other).wait_recv()
 
-    bias = jnp.concatenate([st1[4 * yy + z, 15:16, 0:CB] for yy in range(4)], axis=1)
+    bias = jnp.concatenate([st1[4 * yy + z, 2:3, 0:CB] for yy in range(4)], axis=1)
     CHUNK = 256
 
     def conv_chunk(j, carry):
@@ -413,6 +410,10 @@
 
     conv_chunk(0, 0)
     hid_own(0)
+    x_relay(*qc)
+    when(z != x, lambda: wo_z(z, 0).wait_recv())
+    send(lambda: wo_z(z + 1, 0), (z > x) & (z < 3))
+    send(lambda: wo_z(z - 1, 1), (z < x) & (z > 0))
     conv_chunk(1, 0)
 
     st2s[...] = jnp.zeros_like(st2s)
@@ -434,10 +435,8 @@
     def weights_1():
         x_wait(*qc, 2)
         send(lambda: qd_other(half))
-        wo_y(down, y, 0).wait_recv()
-        send(lambda: wo_y(down, up, 2), c == 0)
-        wo_y(up, y, 1).wait_recv()
-        send(lambda: wo_y(up, down, 2), c == 1)
+        send(lambda: wo_y(y, up, 0))
+        send(lambda: wo_y(y, down, 1))
 
     def second_norm():
         for d in range(1, 16):
@@ -529,10 +528,13 @@
             second_norm()
             qd_other(other).wait_recv()
         if ch == 1:
+            wo_y(down, y, 0).wait_recv()
+            send(lambda: wo_y(down, up, 2), c == 0)
+            wo_y(up, y, 1).wait_recv()
+            send(lambda: wo_y(up, down, 2), c == 1)
+        if ch == 2:
             wo_y(opposite, y, 2).wait_recv()
             x_send(*wox)
-        if ch == 3:
-            x_relay(*wox)
         normalize(ch)
         project(ch)
         kv_own(ch)
@@ -553,8 +555,7 @@
         ref = wo.at[:, :, :, mask]
         return remote(ref, ref, s_wos.at[0], r_wos.at[0], sibling)
 
-    x_wait(*wox, 2)
-    send(lambda: wo_other(half))
+    x_relay(*wox)
     for ch in range(NCH):
         kv_copy(ch, 1, down, y, 0).wait_recv()
         kv_copy(ch, 0, up, y, 1).wait_recv()
@@ -600,7 +601,10 @@
         pl.when(t < 3)(lambda: att_copy(j).start())
         return carry
 
-    lax.fori_loop(0, 4, attend_step, 0)
+    lax.fori_loop(0, 2, attend_step, 0)
+    x_wait(*wox, 2)
+    send(lambda: wo_other(half))
+    lax.fori_loop(2, 4, attend_step, 0)
     attg[z] = att[z]
     for k in range(4):
         pending.append((z != k, lambda k=k: att_copy(k)))
@@ -632,8 +636,8 @@
             pltpu.VMEM((4, CB, C), BF16),
             pltpu.VMEM((3, CZ, C), BF16),
             pltpu.VMEM((4, 4, CB, C), BF16),
-            pltpu.VMEM((32, 128), F32),
-            pltpu.VMEM((16, 32, 128), F32),
+            pltpu.VMEM((8, 128), F32),
+            pltpu.VMEM((16, 8, 128), F32),
             pltpu.VMEM((8, 128), F32),
             pltpu.VMEM((16, 8, 128), F32),
             pltpu.VMEM((C, 128), BF16),

time: 126 us -> 125 us (level); the launches traced: 123 us -> 125 us
    pallas_call x1, Pallas kernels: 122 us -> 123 us  [on_device(): pl.pallas_call(kernel, out_shape=jax.ShapeDtypeStruct((BLK, C), BF16), in...]
where the time goes in v5:
time: 125 us
  Pallas kernels  123 us (98%)
  local copies, waits for them, and re-layouts  1.72 us (1%)
    pallas_call x1, Pallas kernels, on_device(): pl.pallas_call(kernel, out_shape=jax.ShapeDtypeStruct((BLK, C), BF16), in...  123 us

profile of v5, /device:TPU:8, one launch (start us, length us, event | category | flops | bytes accessed | tf_op | source)
XLA Modules:
  0.0 125.2 jit_solution(4250394407296120785)
XLA Ops:
  0.0 123.5 %shard_map.73 = bf16[128,1280]{1,0:T(8,128)(2,1)} custom-call(bf16[128,1280]{1,0:T(8,128)(2,1)} %bitcast.6, bf16[9,80,1280]{2,1,0:T(8,128)(2,1)} %bitcast.4, f32[1,80]{1,0:T(1,128)} %bitcast.7, bf16[80,1280]{1,0:T(8,128)(2,1)} %wq_in.1, bf16[80,1280]{1,0:T(8,128)(2,1)} %wk_in.1, bf16[80,1280]{1,0:T(8,128)(2,1)} %wv_in.1, bf16[80,1280]{1,0:T(8,128)(2,1)} %wo_in.1), custom_call_target="tpu_custom_call" | custom-call | tf_op jit(solution)/shard_map/pallas_call | solution.py:627
  123.5 1.7 %copy.9 = bf16[2,64,1280]{2,1,0:T(8,128)(2,1)} copy(bf16[2,64,1280]{2,1,0:T(8,128)(2,1)} %bitcast.5) | data formatting | bytes 655360

commit v6 on v5

--- a/solution.py
+++ b/solution.py
@@ -172,9 +172,12 @@
 
     nexts = ((x + 1) % 4, (x + 3) % 4, (x + 2) % 4)
 
+    def x_send_if(cond, ref, ssem, rsem):
+        send(lambda: remote(ref(x), ref(x), ssem(0), rsem(1), across(1)), cond)
+        send(lambda: remote(ref(x), ref(x), ssem(1), rsem(0), across(3)), cond)
+
     def x_send(ref, ssem, rsem):
-        send(lambda: remote(ref(x), ref(x), ssem(0), rsem(1), across(1)))
-        send(lambda: remote(ref(x), ref(x), ssem(1), rsem(0), across(3)))
+        x_send_if(None, ref, ssem, rsem)
 
     def x_wait(ref, ssem, rsem, i):
         remote(ref(nexts[i]), ref(nexts[i]), ssem(i), rsem(i), across(1)).wait_recv()
@@ -223,8 +226,6 @@
         ref = wqkv.at[:, :, mask]
         return remote(ref, ref, s_qd.at[0], r_qd.at[0], sibling)
 
-    send(qa_copy, carrier & (z != y))
-    when(carrier & diagonal, lambda: qa_local().start())
     send(lambda: cw_copy(y, up, 0))
     send(lambda: cw_copy(y, down, 1))
 
@@ -245,18 +246,12 @@
         send(lambda: cw_copy(up, down, 2), c == 1)
         for r in range(2):
             send(lambda r=r: cw_other(r, half))
-        when(diagonal & (z != x), lambda: qa_copy().wait_recv())
-        when(diagonal & carrier, lambda: qa_local().wait())
-        send(lambda: qb_copy(up, 0), diagonal)
-        send(lambda: qb_copy(down, 1), diagonal)
         for r in range(2):
             x_relay(*cx(r))
 
     def service_3():
-        beside = (turn == 1) | (turn == 3)
-        when(beside, lambda: qb_copy(up, 0).wait_recv())
-        send(lambda: qb_copy(up, 2), (turn == 1) & (c == 0))
-        send(lambda: qb_copy(down, 2), (turn == 3) & (c == 1))
+        send(qa_copy, carrier & (z != y))
+        when(carrier & diagonal, lambda: qa_local().start())
         x_relay(*cx(2))
 
     services = {1: service_1, 2: service_2, 3: service_3}
@@ -362,8 +357,16 @@
 
     wox = (lambda i: wo.at[:, i, :, half], lambda i: s_wox.at[i], lambda i: r_wox.at[i])
 
-    when(turn == 2, lambda: qb_copy(up, 0).wait_recv())
-    x_send(*qc)
+    when(diagonal & (z != x), lambda: qa_copy().wait_recv())
+    when(diagonal & carrier, lambda: qa_local().wait())
+    send(lambda: qb_copy(up, 0), diagonal)
+    send(lambda: qb_copy(down, 1), diagonal)
+    x_send_if(diagonal, *qc)
+    when(z != x, lambda: wo_z(z, 0).wait_recv())
+    send(lambda: wo_z(z + 1, 0), (z > x) & (z < 3))
+    send(lambda: wo_z(z - 1, 1), (z < x) & (z > 0))
+    send(lambda: wo_y(y, up, 0))
+    send(lambda: wo_y(y, down, 1))
     for r in range(3):
         cw_other(r, other).wait_recv()
         ct_other(r, other).wait_recv()
@@ -410,10 +413,11 @@
 
     conv_chunk(0, 0)
     hid_own(0)
-    x_relay(*qc)
-    when(z != x, lambda: wo_z(z, 0).wait_recv())
-    send(lambda: wo_z(z + 1, 0), (z > x) & (z < 3))
-    send(lambda: wo_z(z - 1, 1), (z < x) & (z > 0))
+    beside = (turn == 1) | (turn == 3)
+    when(beside, lambda: qb_copy(up, 0).wait_recv())
+    send(lambda: qb_copy(up, 2), (turn == 1) & (c == 0))
+    send(lambda: qb_copy(down, 2), (turn == 3) & (c == 1))
+    x_send_if(beside, *qc)
     conv_chunk(1, 0)
 
     st2s[...] = jnp.zeros_like(st2s)
@@ -432,11 +436,12 @@
         )
     st2[p] = st2s[...]
 
-    def weights_1():
-        x_wait(*qc, 2)
-        send(lambda: qd_other(half))
-        send(lambda: wo_y(y, up, 0))
-        send(lambda: wo_y(y, down, 1))
+    when(turn == 2, lambda: qb_copy(up, 0).wait_recv())
+    x_send_if(turn == 2, *qc)
+    wo_y(down, y, 0).wait_recv()
+    send(lambda: wo_y(down, up, 2), c == 0)
+    wo_y(up, y, 1).wait_recv()
+    send(lambda: wo_y(up, down, 2), c == 1)
 
     def second_norm():
         for d in range(1, 16):
@@ -514,32 +519,37 @@
         kv_copy(ch, 1, up, y, 1).wait_recv()
         send(lambda: kv_copy(ch, 1, up, down, 2))
 
-    for ch in range(NCH):
+    def hid_on(ch):
         for k in range(1, 4):
-            when(z - k >= 0, lambda k=k, ch=ch: hid_copy(ch, z - k, 0).wait_recv())
-            send(lambda k=k, ch=ch: hid_copy(ch, z - k, 0), (z - k >= 0) & (z < 3))
-            when(z + k <= 3, lambda k=k, ch=ch: hid_copy(ch, z + k, 1).wait_recv())
-            send(lambda k=k, ch=ch: hid_copy(ch, z + k, 1), (z + k <= 3) & (z > 0))
+            when(z - k >= 0, lambda k=k: hid_copy(ch, z - k, 0).wait_recv())
+            send(lambda k=k: hid_copy(ch, z - k, 0), (z - k >= 0) & (z < 3))
+            when(z + k <= 3, lambda k=k: hid_copy(ch, z + k, 1).wait_recv())
+            send(lambda k=k: hid_copy(ch, z + k, 1), (z + k <= 3) & (z > 0))
             if k == AHEAD and ch + 1 < NCH:
                 hid_own(ch + 1)
-            if ch == 0 and k == 2:
-                weights_1()
-        if ch == 0:
-            second_norm()
-            qd_other(other).wait_recv()
-        if ch == 1:
-            wo_y(down, y, 0).wait_recv()
-            send(lambda: wo_y(down, up, 2), c == 0)
-            wo_y(up, y, 1).wait_recv()
-            send(lambda: wo_y(up, down, 2), c == 1)
-        if ch == 2:
-            wo_y(opposite, y, 2).wait_recv()
-            x_send(*wox)
+
+    def process(ch):
         normalize(ch)
         project(ch)
         kv_own(ch)
         if ch > 0:
             kv_on(ch - 1)
+
+    hid_on(0)
+    x_relay(*qc)
+    hid_on(1)
+    second_norm()
+    x_wait(*qc, 2)
+    send(lambda: qd_other(half))
+    wo_y(opposite, y, 2).wait_recv()
+    x_send(*wox)
+    hid_on(2)
+    qd_other(other).wait_recv()
+    process(0)
+    process(1)
+    hid_on(3)
+    process(2)
+    process(3)
 
     for h in range(2):
         def residual(i, carry, h=h):

time: 125 us -> 120 us (0.960); the launches traced: 125 us -> 119 us
  Pallas kernels: 123 us -> 117 us
    pallas_call x1, Pallas kernels: 123 us -> 117 us  [on_device(): pl.pallas_call(kernel, out_shape=jax.ShapeDtypeStruct((BLK, C), BF16), in...]
where the time goes in v6:
time: 120 us; the launch traced here: 119 us
  Pallas kernels  117 us (98%)
  local copies, waits for them, and re-layouts  1.72 us (1%)
    pallas_call x1, Pallas kernels, on_device(): pl.pallas_call(kernel, out_shape=jax.ShapeDtypeStruct((BLK, C), BF16), in...  117 us

profile of v6, /device:TPU:8, one launch (start us, length us, event | category | flops | bytes accessed | tf_op | source)
XLA Modules:
  0.0 118.5 jit_solution(15217782199651756756)
XLA Ops:
  0.0 116.8 %shard_map.73 = bf16[128,1280]{1,0:T(8,128)(2,1)} custom-call(bf16[128,1280]{1,0:T(8,128)(2,1)} %bitcast.6, bf16[9,80,1280]{2,1,0:T(8,128)(2,1)} %bitcast.4, f32[1,80]{1,0:T(1,128)} %bitcast.7, bf16[80,1280]{1,0:T(8,128)(2,1)} %wq_in.1, bf16[80,1280]{1,0:T(8,128)(2,1)} %wk_in.1, bf16[80,1280]{1,0:T(8,128)(2,1)} %wv_in.1, bf16[80,1280]{1,0:T(8,128)(2,1)} %wo_in.1), custom_call_target="tpu_custom_call" | custom-call | tf_op jit(solution)/shard_map/pallas_call | solution.py:637
  116.8 1.7 %copy.9 = bf16[2,64,1280]{2,1,0:T(8,128)(2,1)} copy(bf16[2,64,1280]{2,1,0:T(8,128)(2,1)} %bitcast.5) | data formatting | bytes 655360

commit v7 on v6

--- a/solution.py
+++ b/solution.py
@@ -246,12 +246,12 @@
         send(lambda: cw_copy(up, down, 2), c == 1)
         for r in range(2):
             send(lambda r=r: cw_other(r, half))
+        send(qa_copy, carrier & (z != y))
+        when(carrier & diagonal, lambda: qa_local().start())
         for r in range(2):
             x_relay(*cx(r))
 
     def service_3():
-        send(qa_copy, carrier & (z != y))
-        when(carrier & diagonal, lambda: qa_local().start())
         x_relay(*cx(2))
 
     services = {1: service_1, 2: service_2, 3: service_3}
@@ -346,6 +346,11 @@
     when(y == 0, zero_top)
     when(y == 3, zero_bottom)
 
+    when(diagonal & (z != x), lambda: qa_copy().wait_recv())
+    when(diagonal & carrier, lambda: qa_local().wait())
+    send(lambda: qb_copy(up, 0), diagonal)
+    send(lambda: qb_copy(down, 1), diagonal)
+    x_send_if(diagonal, *qc)
     cw_copy(opposite, y, 2).wait_recv()
     send(lambda: cw_other(2, half))
     for r in range(3):
@@ -357,16 +362,6 @@
 
     wox = (lambda i: wo.at[:, i, :, half], lambda i: s_wox.at[i], lambda i: r_wox.at[i])
 
-    when(diagonal & (z != x), lambda: qa_copy().wait_recv())
-    when(diagonal & carrier, lambda: qa_local().wait())
-    send(lambda: qb_copy(up, 0), diagonal)
-    send(lambda: qb_copy(down, 1), diagonal)
-    x_send_if(diagonal, *qc)
-    when(z != x, lambda: wo_z(z, 0).wait_recv())
-    send(lambda: wo_z(z + 1, 0), (z > x) & (z < 3))
-    send(lambda: wo_z(z - 1, 1), (z < x) & (z > 0))
-    send(lambda: wo_y(y, up, 0))
-    send(lambda: wo_y(y, down, 1))
     for r in range(3):
         cw_other(r, other).wait_recv()
         ct_other(r, other).wait_recv()
@@ -438,10 +433,11 @@
 
     when(turn == 2, lambda: qb_copy(up, 0).wait_recv())
     x_send_if(turn == 2, *qc)
-    wo_y(down, y, 0).wait_recv()
-    send(lambda: wo_y(down, up, 2), c == 0)
-    wo_y(up, y, 1).wait_recv()
-    send(lambda: wo_y(up, down, 2), c == 1)
+    when(z != x, lambda: wo_z(z, 0).wait_recv())
+    send(lambda: wo_z(z + 1, 0), (z > x) & (z < 3))
+    send(lambda: wo_z(z - 1, 1), (z < x) & (z > 0))
+    send(lambda: wo_y(y, up, 0))
+    send(lambda: wo_y(y, down, 1))
 
     def second_norm():
         for d in range(1, 16):
@@ -541,9 +537,13 @@
     second_norm()
     x_wait(*qc, 2)
     send(lambda: qd_other(half))
+    wo_y(down, y, 0).wait_recv()
+    send(lambda: wo_y(down, up, 2), c == 0)
+    wo_y(up, y, 1).wait_recv()
+    send(lambda: wo_y(up, down, 2), c == 1)
+    hid_on(2)
     wo_y(opposite, y, 2).wait_recv()
     x_send(*wox)
-    hid_on(2)
     qd_other(other).wait_recv()
     process(0)
     process(1)

time: 120 us -> 116 us (0.967)
  Pallas kernels: 117 us -> 113 us
    pallas_call x1, Pallas kernels: 117 us -> 113 us  [on_device(): pl.pallas_call(kernel, out_shape=jax.ShapeDtypeStruct((BLK, C), BF16), in...]
where the time goes in v7:
time: 116 us; the launch traced here: 115 us
  Pallas kernels  113 us (97%)
  local copies, waits for them, and re-layouts  1.72 us (1%)
    pallas_call x1, Pallas kernels, on_device(): pl.pallas_call(kernel, out_shape=jax.ShapeDtypeStruct((BLK, C), BF16), in...  113 us

profile of v7, /device:TPU:8, one launch (start us, length us, event | category | flops | bytes accessed | tf_op | source)
XLA Modules:
  0.0 114.8 jit_solution(10060298241999482834)
XLA Ops:
  0.0 113.1 %shard_map.73 = bf16[128,1280]{1,0:T(8,128)(2,1)} custom-call(bf16[128,1280]{1,0:T(8,128)(2,1)} %bitcast.6, bf16[9,80,1280]{2,1,0:T(8,128)(2,1)} %bitcast.4, f32[1,80]{1,0:T(1,128)} %bitcast.7, bf16[80,1280]{1,0:T(8,128)(2,1)} %wq_in.1, bf16[80,1280]{1,0:T(8,128)(2,1)} %wk_in.1, bf16[80,1280]{1,0:T(8,128)(2,1)} %wv_in.1, bf16[80,1280]{1,0:T(8,128)(2,1)} %wo_in.1), custom_call_target="tpu_custom_call" | custom-call | tf_op jit(solution)/shard_map/pallas_call | solution.py:637
  113.1 1.7 %copy.9 = bf16[2,64,1280]{2,1,0:T(8,128)(2,1)} copy(bf16[2,64,1280]{2,1,0:T(8,128)(2,1)} %bitcast.5) | data formatting | bytes 655360

commit v8 on v7

--- a/solution.py
+++ b/solution.py
@@ -36,7 +36,7 @@
 def kernel(
     lat_in, cw_in, bias_in, wq_in, wk_in, wv_in, wo_in, out_ref,
     lat, act, cw, wown, wqkv, wo, st1s, st1, st2s, st2, gmat, gmat_t, sel,
-    gn1, gn2, stc, ubuf, hidg, nrm, hnat, qb, kv, att, attg,
+    gn1, gn2, stc, peaks, totals, mixes, ubuf, hidg, nrm, hnat, qb, kv, att, attg,
     s_loc, s_st1, r_st1, s_lat, r_lat, s_halo, r_halo, s_cw, r_cw, s_cws, r_cws,
     s_ct, r_ct, s_cx, r_cx, s_cts, r_cts,
     s_qa, r_qa, l_qa, s_qb, r_qb, s_qc, r_qc, s_qd, r_qd, s_woz, r_woz, s_woy, r_woy, s_wox, r_wox, s_wos, r_wos,
@@ -569,8 +569,6 @@
     for ch in range(NCH):
         kv_copy(ch, 1, down, y, 0).wait_recv()
         kv_copy(ch, 0, up, y, 1).wait_recv()
-        kv_copy(ch, 0, opposite, y, 2).wait_recv()
-        kv_copy(ch, 1, opposite, y, 2).wait_recv()
 
     def att_copy(j):
         return remote(att.at[j], attg.at[z], s_att.at[j], r_att.at[z], patch(y, j))
@@ -578,32 +576,52 @@
     def att_from(k):
         return remote(att.at[k], attg.at[k], s_att.at[k], r_att.at[k], patch(y, k))
 
+    def softmax_part(rows, pair, side, blocks):
+        key_at = 128 * pair if pair < 2 else 512
+        value_at = key_at + 256 if pair < 2 else 512
+        query = qb[rows, 128 * pair : 128 * pair + 128]
+        if pair < 2:
+            lane = lax.broadcasted_iota(jnp.int32, (BLK, 128), 1)
+            keep = (lane >= 64 * side) & (lane < 64 * side + 64)
+            query = jnp.where(keep, query.astype(F32), 0.0).astype(BF16)
+        scores = [dot_nt(query, kv[i, :, key_at : key_at + 128]) for i in blocks]
+        peak = jnp.max(scores[0], axis=1, keepdims=True)
+        for one in scores[1:]:
+            peak = jnp.maximum(peak, jnp.max(one, axis=1, keepdims=True))
+        total, mix = None, None
+        for i, one in zip(blocks, scores):
+            unnormalized = jnp.exp(one - peak)
+            part = jnp.sum(unnormalized, axis=1, keepdims=True)
+            value = dot_nn(unnormalized.astype(BF16), kv[i, :, value_at : value_at + 128])
+            total = part if total is None else total + part
+            mix = value if mix is None else mix + value
+        return peak, total, mix
+
+    heads = [(0, 0), (0, 1), (1, 0), (1, 1), (2, 0)]
+
+    def attend_first(j, carry):
+        rows = pl.ds(pl.multiple_of(BLK * j, 128), BLK)
+        for h, (pair, side) in enumerate(heads):
+            peak, total, mix = softmax_part(rows, pair, side, (y, down, up))
+            peaks[h, rows, :] = peak
+            totals[h, rows, :] = total
+            mixes[h, rows, :] = mix
+        return carry
+
     def attend(j):
         rows = pl.ds(pl.multiple_of(BLK * j, 128), BLK)
-        for pair in range(3):
-            width = min(128, CZ - 128 * pair)
-            lanes = slice(128 * pair, 128 * pair + width)
-            query = qb[rows, 128 * pair : 128 * pair + 128]
-            key_at = 128 * pair if pair < 2 else 512
-            value_at = key_at + 256 if pair < 2 else 512
-            keys = kv[:, :, key_at : key_at + 128].reshape(2048, 128)
-            values = kv[:, :, value_at : value_at + 128].reshape(2048, 128)
-            lane = lax.broadcasted_iota(jnp.int32, (BLK, 128), 1)
-            result = None
-            for side in range(width // 64):
-                q1 = query
-                if width > 64:
-                    keep = (lane >= 64 * side) & (lane < 64 * side + 64)
-                    q1 = jnp.where(keep, query.astype(F32), 0.0).astype(BF16)
-                scores = dot_nt(q1, keys)
-                peak = jnp.max(scores, axis=1, keepdims=True)
-                unnormalized = jnp.exp(scores - peak)
-                row_total = jnp.sum(unnormalized, axis=1, keepdims=True)
-                mix = dot_nn(unnormalized.astype(BF16), values) / row_total
-                result = mix if result is None else jnp.where(lane < 64, result, mix)
-            if width == 64:
-                result = result[:, 64:128]
-            att[j, :, lanes] = result.astype(BF16)
+        lane = lax.broadcasted_iota(jnp.int32, (BLK, 128), 1)
+        done = []
+        for h, (pair, side) in enumerate(heads):
+            peak, total, mix = softmax_part(rows, pair, side, (opposite,))
+            before = peaks[h, rows, :]
+            peak_all = jnp.maximum(before, peak)
+            old, new = jnp.exp(before - peak_all), jnp.exp(peak - peak_all)
+            row_total = old * totals[h, rows, :] + new * total
+            done.append((old * mixes[h, rows, :] + new * mix) / row_total)
+        att[j, :, 0:128] = jnp.where(lane < 64, done[0], done[1]).astype(BF16)
+        att[j, :, 128:256] = jnp.where(lane < 64, done[2], done[3]).astype(BF16)
+        att[j, :, 256:CZ] = done[4][:, 64:128].astype(BF16)
 
     def attend_step(t, carry):
         j = (z + 1 + t) % 4
@@ -611,10 +629,13 @@
         pl.when(t < 3)(lambda: att_copy(j).start())
         return carry
 
-    lax.fori_loop(0, 2, attend_step, 0)
+    lax.fori_loop(0, 4, attend_first, 0)
     x_wait(*wox, 2)
     send(lambda: wo_other(half))
-    lax.fori_loop(2, 4, attend_step, 0)
+    for ch in range(NCH):
+        kv_copy(ch, 0, opposite, y, 2).wait_recv()
+        kv_copy(ch, 1, opposite, y, 2).wait_recv()
+    lax.fori_loop(0, 4, attend_step, 0)
     attg[z] = att[z]
     for k in range(4):
         pending.append((z != k, lambda k=k: att_copy(k)))
@@ -656,6 +677,9 @@
             pltpu.VMEM((2, 8, C), F32),
             pltpu.VMEM((2, 8, CZ), F32),
             pltpu.VMEM((2, 8, CZ), F32),
+            pltpu.VMEM((5, ROWS_Y, 1), F32),
+            pltpu.VMEM((5, ROWS_Y, 1), F32),
+            pltpu.VMEM((5, ROWS_Y, 128), F32),
             pltpu.VMEM((256, 3 * CZ), F32),
             pltpu.VMEM((4, NCH, 5, HALF, 128), BF16),
             pltpu.VMEM((R, C), BF16),

time: 116 us -> 121 us (1.043)
  Pallas kernels: 113 us -> 118 us
    pallas_call x1, Pallas kernels: 113 us -> 118 us  [on_device(): pl.pallas_call(kernel, out_shape=jax.ShapeDtypeStruct((BLK, C), BF16), in...]
where the time goes in v8:
time: 121 us; the launch traced here: 120 us
  Pallas kernels  118 us (98%)
  local copies, waits for them, and re-layouts  1.72 us (1%)
    pallas_call x1, Pallas kernels, on_device(): pl.pallas_call(kernel, out_shape=jax.ShapeDtypeStruct((BLK, C), BF16), in...  118 us

profile of v8, /device:TPU:8, one launch (start us, length us, event | category | flops | bytes accessed | tf_op | source)
XLA Modules:
  0.0 120.0 jit_solution(1989678790762925474)
XLA Ops:
  0.0 118.3 %shard_map.73 = bf16[128,1280]{1,0:T(8,128)(2,1)} custom-call(bf16[128,1280]{1,0:T(8,128)(2,1)} %bitcast.6, bf16[9,80,1280]{2,1,0:T(8,128)(2,1)} %bitcast.4, f32[1,80]{1,0:T(1,128)} %bitcast.7, bf16[80,1280]{1,0:T(8,128)(2,1)} %wq_in.1, bf16[80,1280]{1,0:T(8,128)(2,1)} %wk_in.1, bf16[80,1280]{1,0:T(8,128)(2,1)} %wv_in.1, bf16[80,1280]{1,0:T(8,128)(2,1)} %wo_in.1), custom_call_target="tpu_custom_call" | custom-call | tf_op jit(solution)/shard_map/pallas_call | solution.py:658
  118.3 1.7 %copy.9 = bf16[2,64,1280]{2,1,0:T(8,128)(2,1)} copy(bf16[2,64,1280]{2,1,0:T(8,128)(2,1)} %bitcast.5) | data formatting | bytes 655360

commit v9 on v7

--- a/solution.py
+++ b/solution.py
@@ -534,9 +534,9 @@
     hid_on(0)
     x_relay(*qc)
     hid_on(1)
-    second_norm()
     x_wait(*qc, 2)
     send(lambda: qd_other(half))
+    second_norm()
     wo_y(down, y, 0).wait_recv()
     send(lambda: wo_y(down, up, 2), c == 0)
     wo_y(up, y, 1).wait_recv()
@@ -551,6 +551,8 @@
     process(2)
     process(3)
 
+    kv_on(NCH - 1)
+
     for h in range(2):
         def residual(i, carry, h=h):
             rows = pl.ds(pl.multiple_of(16 * i, 16), 16)
@@ -560,7 +562,6 @@
 
         lax.fori_loop(0, HALF // 16, residual, 0)
 
-    kv_on(NCH - 1)
     def wo_other(mask):
         ref = wo.at[:, :, :, mask]
         return remote(ref, ref, s_wos.at[0], r_wos.at[0], sibling)

time: 116 us -> 116 us (level)
  no operation moved by 1% of the time
where the time goes in v9:
time: 116 us; the launch traced here: 115 us
  Pallas kernels  113 us (97%)
  local copies, waits for them, and re-layouts  1.72 us (1%)
    pallas_call x1, Pallas kernels, on_device(): pl.pallas_call(kernel, out_shape=jax.ShapeDtypeStruct((BLK, C), BF16), in...  113 us

profile of v9, /device:TPU:8, one launch (start us, length us, event | category | flops | bytes accessed | tf_op | source)
XLA Modules:
  0.0 114.8 jit_solution(2516646856589738529)
XLA Ops:
  0.0 113.1 %shard_map.73 = bf16[128,1280]{1,0:T(8,128)(2,1)} custom-call(bf16[128,1280]{1,0:T(8,128)(2,1)} %bitcast.6, bf16[9,80,1280]{2,1,0:T(8,128)(2,1)} %bitcast.4, f32[1,80]{1,0:T(1,128)} %bitcast.7, bf16[80,1280]{1,0:T(8,128)(2,1)} %wq_in.1, bf16[80,1280]{1,0:T(8,128)(2,1)} %wk_in.1, bf16[80,1280]{1,0:T(8,128)(2,1)} %wv_in.1, bf16[80,1280]{1,0:T(8,128)(2,1)} %wo_in.1), custom_call_target="tpu_custom_call" | custom-call | tf_op jit(solution)/shard_map/pallas_call | solution.py:638
  113.1 1.7 %copy.9 = bf16[2,64,1280]{2,1,0:T(8,128)(2,1)} copy(bf16[2,64,1280]{2,1,0:T(8,128)(2,1)} %bitcast.5) | data formatting | bytes 655360
